TPU v7x, 256 devices: a whole 4x4x8 slice. The times are simulated.
256 devices in a mesh: grp: 2 (over x_hi), fsdp: 128 (over z, y, x_lo, core).
Axes of the slice: x: 4 (x_hi: 2, x_lo: 2; x = x_hi * 2 + x_lo), y: 4, z: 8, core: 2. Of those that a mesh axis runs over, the one named last changes fastest.
Arguments:
- token_states: bfloat16 [2, 384, 128, 4096], P('grp', 'fsdp'), may hold values from -250 to 250
- token_ids: int32 [2, 384, 128], P('grp', 'fsdp'), may hold values from 0 to 31999, as said below
- master: float32 [2, 4096, 1024], P('grp', 'fsdp'), may hold values from -0.09375 to 0.09375
- gain: float32 [4096], replicated, may hold values from 0.25 to 4.5
- cand_ids: int32 [384, 8], P('fsdp'), may hold values from 0 to 383, all different within a row
- slab_owner: int32 [384], replicated, may hold values from 0 to 127, as said below
Outputs:
- weights_out: float32 [2, 4096, 1024], P('grp', 'fsdp')
Inputs may be any that keep to these rules, and one draw needn't show every extreme that they name: `token_ids`: 0 marks padding, which only follows a sequence's tokens; every sequence has 16 or more tokens. `slab_owner`: each fsdp index owns exactly 3 slab rows; the passages of slot 1 on the device with that index are the rows it owns, in increasing order. `cand_ids`: the ids of one row differ, and every slab row is some query's candidate.
All inputs are finite; a program needn't handle non-finite values.
Results may differ from a plain program's by a relative error of at most 0.012.
The roundings to bfloat16 on the way count: a program that leaves them out, or rounds other values in their place, can miss the bound.
Values may be sent and summed in bfloat16 or wider, within the bound.
A program may use at most 64 MiB of HBM per device.

v0:
```python
import jax
import jax.numpy as jnp
from jax import lax
from jax.sharding import PartitionSpec as P

sharpness = 20.0


def passed_along(shard, axis, by):
    size = lax.axis_size(axis)
    pairs = [(i, i + by) for i in range(size) if 0 <= i + by < size]
    return lax.ppermute(shard, axis, pairs)


def shards(token_states, token_ids, master, gain, cand_ids, slab_owner):
    trainer = lax.axis_index("grp") == 0
    devices_fsdp = lax.axis_size("fsdp")
    states = token_states[0]
    seq_dev, length, width = states.shape
    embedding = master.shape[2]
    shard_rows = master.shape[1]
    tokens_dev = seq_dev * length
    states_wide = states.astype(jnp.float32)
    mean_square = jnp.mean(states_wide * states_wide, axis=-1, keepdims=True)
    normed = (
        (states_wide * lax.rsqrt(mean_square + 1e-05) * gain)
        .astype(jnp.bfloat16)
        .reshape(tokens_dev, width)
    )
    weight_bf = master[0].astype(jnp.bfloat16)
    hidden = jnp.dot(
        normed,
        lax.all_gather(weight_bf, "fsdp", axis=0, tiled=True),
        preferred_element_type=jnp.float32,
    )
    copied = passed_along(weight_bf, "grp", 1)
    active = jnp.tanh(hidden).reshape(seq_dev, length, embedding)
    valid = (token_ids[0] != 0).astype(jnp.float32)
    counts = jnp.sum(valid, axis=1)
    pooled = jnp.sum(active * valid[:, :, None], axis=1) / counts[:, None]
    pooled_square = jnp.mean(pooled * pooled, axis=-1, keepdims=True)
    scale = lax.rsqrt(pooled_square + 1e-06)
    unit = pooled * scale
    stored = unit.astype(jnp.bfloat16)
    owners = jnp.arange(devices_fsdp, dtype=jnp.int32)
    onehot = (slab_owner[:, None] == owners[None, :]).astype(jnp.int32)
    ranks = jnp.sum((jnp.cumsum(onehot, axis=0) - onehot) * onehot, axis=1)
    places = slab_owner * seq_dev + ranks
    wanted = places[cand_ids]
    whole = lax.all_gather(stored, "fsdp", axis=0, tiled=True)
    slab = passed_along(whole, "grp", -1)
    chosen = slab[wanted]
    chosen_wide = chosen.astype(jnp.float32)
    logits = (
        sharpness
        / embedding
        * jnp.einsum("qe,qje->qj", unit, chosen_wide, precision=lax.Precision.HIGHEST)
    )
    exponent = jnp.exp(logits)
    probs = exponent / jnp.sum(exponent, axis=-1, keepdims=True)
    target = (jnp.arange(chosen.shape[1]) == 0).astype(jnp.float32)
    logit_grad = probs - target[None, :]
    unit_grad = (
        sharpness
        / embedding
        * jnp.einsum("qj,qje->qe", logit_grad, chosen_wide, precision=lax.Precision.HIGHEST)
    )
    inner = jnp.sum(pooled * unit_grad, axis=-1, keepdims=True)
    pooled_grad = scale * unit_grad - pooled * (scale * scale * scale) * inner / embedding
    delta = (
        (valid / counts[:, None])[:, :, None] * pooled_grad[:, None, :] * (1.0 - active * active)
    )
    delta = delta.astype(jnp.bfloat16).reshape(tokens_dev, embedding)

    def compute():
        return lax.dot_general(
            normed, delta, (((0,), (0,)), ((), ())), preferred_element_type=jnp.float32
        )

    shard = lax.psum_scatter(
        lax.cond(
            trainer,
            compute,
            lambda: jnp.zeros((lax.axis_size("fsdp") * shard_rows, embedding), jnp.float32),
        ),
        "fsdp",
        scatter_dimension=0,
        tiled=True,
    )
    row_square = jnp.mean(shard * shard, axis=1, keepdims=True)
    normalized = shard * lax.rsqrt(row_square + 1e-06)
    result = jnp.where(trainer, normalized, copied.astype(jnp.float32))
    return result[None]


def solution(mesh):
    placed = (
        P("grp", "fsdp", None, None),
        P("grp", "fsdp", None),
        P("grp", "fsdp", None),
        P(),
        P("fsdp", None),
        P(),
    )
    return jax.shard_map(
        shards, mesh=mesh, in_specs=placed, out_specs=P("grp", "fsdp", None), check_vma=False
    )
```

profile of v0, /device:TPU:8, one launch (start us, length us, event | category | flops | bytes accessed | tf_op | source)
XLA Modules:
  0.0 1037.1 jit_solution(8004294407138557702)
XLA Ops:
  6.5 0.0 all-gather.4.cloned.1.call-start
  6.5 1.7 convert_element_type.74
  8.2 0.0 all-gather.4.cloned.1.call-update
  8.3 0.0 reduce-scatter.2.cloned.1.call-start
  8.3 0.7 compare_convert_fusion
  9.0 0.8 copy.11
  9.8 0.2 fusion.9
  10.1 0.7 compare_select_fusion.1
  10.8 0.1 reshape.125
  10.9 0.9 fusion.12
  11.8 0.7 multiply_add_fusion
  12.5 0.7 gather_fusion
  13.2 0.1 gather.9
  13.3 0.0 copy-done.5
  13.3 0.1 fusion.27
  13.4 0.7 multiply_reduce_fusion
  14.1 0.0 copy-done.4
  14.1 1.1 copy-done.1
  15.2 1.2 fusion.3
  16.4 213.2 %all-gather.4.cloned.1.call-done = bf16[1,4096,1024]{2,1,0:T(8,128)(2,1)} async-done(((bf16[1,32,1024]{2,1,0:T(8,128)(2,1)}), bf16[1,4096,1024]{2,1,0:T(8,128)(2,1)}) %all-gather.4.cloned.1.call-update) | async-done | bytes 8388624 | tf_op jit(solution)/shard_map/all_gather | solution.py:33
  229.6 5.8 fusion.6
  235.4 1.1 copy-done.2
  236.5 0.2 multiply_reduce_fusion.1
  236.7 0.2 multiply_reduce_fusion.3
  236.9 0.1 multiply_bitcast_fusion
  237.0 163.8 %all-gather.1 = bf16[128,3,1024]{2,1,0:T(4,128)(2,1)} all-gather(bf16[1,3,1024]{2,1,0:T(4,128)(2,1)S(1)} %get-tuple-element.21), channel_id=1, replica_groups=mesh['grp'=2,'fsdp'=128] {'fsdp'}, dimensions={0}, use_global_device_ids=true | all-gather | bytes 792576 | tf_op jit(solution)/shard_map/all_gather | solution.py:50
  400.8 3.2 reshape.145
  404.0 1.3 collective-permute-start
  405.3 0.1 reshape.133
  405.4 0.1 bitcast_divide_fusion
  405.5 22.0 %collective-permute-done = bf16[384,1024]{1,0:T(8,128)(2,1)} collective-permute-done((bf16[384,1024]{1,0:T(8,128)(2,1)}, bf16[384,1024]{1,0:T(8,128)(2,1)}, u32[]{:S(2)}, u32[]{:S(2)}) %collective-permute-start) | collective-permute-done | bytes 786464 | tf_op jit(solution)/shard_map/ppermute | solution.py:12
  427.5 1.9 gather_fusion.1
  429.4 0.2 fusion.14
  429.6 0.1 fusion.24
  429.7 0.1 subtract_bitcast_fusion
  429.8 0.2 fusion.16
  430.0 0.1 fusion.20
  430.1 0.1 fusion.18
  430.2 2.6 fusion.5
  432.8 9.2 conditional.1
  432.8 9.2 fusion.28
  442.0 0.0 reduce-scatter.2.cloned.1.call-update
  442.0 0.9 copy-done.3
  442.9 1.3 collective-permute-start.1
  444.2 583.4 %reduce-scatter.2.cloned.1.call-done = f32[32,1024]{1,0:T(8,128)} async-done(((f32[4096,1024]{1,0:T(8,128)}), f32[32,1024]{1,0:T(8,128)}) %reduce-scatter.2.cloned.1.call-update) | async-done | bytes 131088 | tf_op jit(solution)/shard_map/reduce_scatter | solution.py:80
  1027.6 1.0 multiply_reduce_fusion.2
  1028.6 0.0 collective-permute-done.1
  1028.6 1.6 select_bitcast_fusion
  (21 shorter events, 0.2 us)
Async XLA Ops:
  6.5 6.8 copy-start.5
  6.5 6.9 copy-start
  6.5 223.0 %all-gather.4.cloned.1.call-start = ((), (), s32[]{:S(2)}) async-start(), calls=%async_computation.2 | async-start | bytes 8454144 | tf_op jit(solution)/shard_map/all_gather | solution.py:33
  8.3 1019.3 %reduce-scatter.2.cloned.1.call-start = ((), (), s32[]{:S(2)}) async-start(), calls=%async_computation.1 | async-start | bytes 16908288 | tf_op jit(solution)/shard_map/reduce_scatter | solution.py:80
  10.0 4.1 copy-start.4
  13.3 1.9 copy-start.1
  235.4 1.2 copy-start.2
  404.0 23.5 %collective-permute-start = (bf16[384,1024]{1,0:T(8,128)(2,1)}, bf16[384,1024]{1,0:T(8,128)(2,1)}, u32[]{:S(2)}, u32[]{:S(2)}) collective-permute-start(bf16[384,1024]{1,0:T(8,128)(2,1)} %reshape.145), channel_id=1, source_target_pairs={{128,0},{129,1},{130,2},{131,3},{132,4},{133,5},{134,6},{135,7},{1... | collective-permute-start | bytes 2359304 | tf_op jit(solution)/shard_map/ppermute | solution.py:12
  442.0 0.9 copy-start.3
  442.9 585.7 %collective-permute-start.1 = (bf16[32,1024]{1,0:T(8,128)(2,1)S(1)}, bf16[32,1024]{1,0:T(8,128)(2,1)S(1)}, u32[]{:S(2)}, u32[]{:S(2)}) collective-permute-start(bf16[32,1024]{1,0:T(8,128)(2,1)S(1)} %convert_bitcast_fusion), channel_id=1, source_target_pairs={{0,128},{1,129},{2,130},{3,131},{4,132},{5,133},{6,134},{7,135},{8... | collective-permute-start | bytes 196616 | tf_op jit(solution)/shard_map/ppermute | solution.py:12
Sparse Core Ops, SparseCore 0:
  9.2 220.3 all-gather.3
  442.1 585.3 reduce-scatter.1
where the time goes:
time: 1050 us; the launch traced here: 1040 us
  waiting for transfers between devices  819 us (78%)
  blocking collectives  164 us (16%)
  matrix products  15.4 us (1%)
  between operations  13.5 us (1%)
  other arithmetic  13.1 us (1%)
    reduce_scatter x1, waiting for transfers between devices, shards(): lax.psum_scatter(lax.cond(trainer, compute, lambda: jnp.zeros((lax.axis_s...  583 us
    all_gather x1, waiting for transfers between devices, shards(): lax.all_gather(weight_bf, 'fsdp', axis=0, tiled=True)  213 us
    all_gather x1, blocking collectives, shards(): whole = lax.all_gather(stored, 'fsdp', axis=0, tiled=True)  164 us
    ppermute x2, waiting for transfers between devices, passed_along(): return lax.ppermute(shard, axis, pairs)  22 us
  transfers between devices with their start and end apart: 4, of which 3 were waited for; matrix products, arithmetic and copies ran while one was open for 1% of the time, Pallas kernels for 0%

commit v1 on v0

v1 whole, which is shorter than its diff:
```python
import jax
import jax.numpy as jnp
from jax import lax
from jax.experimental import pallas as pl
from jax.experimental.pallas import tpu as pltpu
from jax.sharding import PartitionSpec as P

MESH = pl.DeviceIdType.MESH
SHARPNESS = 20.0
NZ, NY = 8, 4
BF, F32 = jnp.bfloat16, jnp.float32
OFFS = (0, -1, 1, -2, 2, -3, 3, 4)
RS_OFFS = (4, 3, -3, 2, -2, 1, -1, 0)
J_ORDER = (0, 1, 3, 2)


def body(
    states_hbm, ids_ref, master_ref, gain_ref, owner_ref, cand_s, owner_s, out_ref,
    states, normed, trans, trans_peer, weight, wrecv, act, stage, stored, slab,
    delta, delta_peer, part, total, big_s, big_r, small_s, small_r, piece_s, piece_r, place_s,
    st_sem, ag_s, ag_r, zr_s, zr_r, yr_s, yr_r, fw_s, fw_r, wt_s, wt_r, tp_s, tp_r,
    e1_s, e1_r, e2_s, e2_r, e3_s, e3_r, dl_s, dl_r, bg_ss, bg_rs, sm_ss, sm_rs, pc_ss, pc_rs,
):
    g = lax.axis_index("grp")
    f = lax.axis_index("fsdp")
    c = f % 2
    x = (f // 2) % 2
    y = (f // 4) % NY
    z = f // 16
    tokens, width = states.shape
    emb = weight.shape[-1]

    def dev(zz, yy, xx, cc, gg=None):
        index = (((zz % NZ) * NY + yy % NY) * 2 + xx) * 2 + cc
        return (g if gg is None else gg, index)

    def copy(src, dst, ssem, rsem, to):
        return pltpu.make_async_remote_copy(
            src_ref=src, dst_ref=dst, send_sem=ssem, recv_sem=rsem,
            device_id=to, device_id_type=MESH,
        )

    me = (g, f)
    partner = dev(z, y, x, 1 - c)

    load = pltpu.make_async_copy(states_hbm, states, st_sem)
    load.start()
    weight[z, y, x, c] = master_ref[...].astype(BF)

    barrier = pltpu.get_barrier_semaphore()
    peers = [dev(z, y + dy, (x + dx) % 2, c) for dy in range(NY) for dx in range(2) if dy or dx]
    peers += [dev(z + 1, y, x, c), dev(z - 1, y, x, c), partner]
    peers += [dev(zz, y, x, c, 1 - g) for zz in range(NZ)]
    for peer in peers:
        pl.semaphore_signal(barrier, inc=1, device_id=peer, device_id_type=MESH)
    pl.semaphore_wait(barrier, len(peers))

    def shard(zz, yy, xx, cc):
        return weight.at[zz % NZ, yy % NY, xx, cc]

    def chunk(zz, yy, cc):
        return weight.at[zz % NZ, yy % NY, :, cc]

    def forward(zz, yy, cc):
        k = (zz % NZ) * NY + yy % NY
        ref = chunk(zz, yy, cc)
        copy(ref, ref, fw_s.at[k], fw_r.at[k], partner).start()

    def send_chunk(ref, ssem, rsem, to):
        copy(ref, ref, ssem, rsem, to).start()

    def got(ref, ssem, rsem):
        copy(ref, ref, ssem, rsem, me).wait_recv()

    def sent(ref, ssem, rsem):
        copy(ref, ref, ssem, rsem, me).wait_send()

    own = shard(z, y, x, c)

    def norm_step(i, carry):
        rows = pl.ds(pl.multiple_of(i * 16, 16), 16)
        wide = states[rows, :].astype(F32)
        mean_square = jnp.sum(wide * wide, axis=-1, keepdims=True) * (1.0 / width)
        normed[rows, :] = (wide * lax.rsqrt(mean_square + 1e-05) * gain_ref[...]).astype(BF)
        return carry

    def norm():
        load.wait()
        lax.fori_loop(0, tokens // 16, norm_step, 0)

    def transpose_step(i, carry):
        columns = pl.ds(pl.multiple_of(i * 512, 512), 512)
        turned = jnp.transpose(normed[:, columns])
        trans[i] = turned.reshape(NY, 2, 2, 32, tokens)
        return carry

    def transpose(lo, hi):
        lax.fori_loop(lo, hi, transpose_step, 0)

    trainer = g == 0

    def weight_copy():
        return copy(own, wrecv, wt_s, wt_r, (1 - g, f))

    @pl.when(trainer)
    def _():
        weight_copy().start()

    @pl.when(c == 0)
    def _():
        for dy in range(NY):
            for dx in range(2):
                if dy or dx:
                    k = dy * 2 + dx
                    send_chunk(own, ag_s.at[k], ag_r.at[k], dev(z, y + dy, (x + dx) % 2, 0))
        norm()
        step = (1, -1)
        for j in J_ORDER:
            yj = y + j
            for dx in range(2):
                if j or dx:
                    k = ((-j) % NY) * 2 + dx
                    got(shard(z, yj, (x + dx) % 2, 0), ag_s.at[k], ag_r.at[k])
            for d in range(2):
                send_chunk(chunk(z, yj, 0), zr_s.at[d, 0, j], zr_r.at[d, 0, j], dev(z + step[d], y, x, 0))
            forward(z, yj, 0)
        transpose(0, 2)
        for s in range(2, 5):
            for j in J_ORDER:
                yj = y + j
                for d in range(2):
                    zz = z - step[d] * (s - 1)
                    got(chunk(zz, yj, 0), zr_s.at[d, s - 2, j], zr_r.at[d, s - 2, j])
                    if s < 4 or (j % 2) == d:
                        send_chunk(
                            chunk(zz, yj, 0), zr_s.at[d, s - 1, j], zr_r.at[d, s - 1, j],
                            dev(z + step[d], y, x, 0),
                        )
                    forward(zz, yj, 0)
            transpose(2 * s - 2, 2 * s)
        for j in J_ORDER:
            d = j % 2
            got(chunk(z + 4, y + j, 0), zr_s.at[d, 3, j], zr_r.at[d, 3, j])
            forward(z + 4, y + j, 0)
        for dy in range(NY):
            for dx in range(2):
                if dy or dx:
                    k = dy * 2 + dx
                    sent(own, ag_s.at[k], ag_r.at[k])
        for s in range(1, 5):
            for j in range(NY):
                for d in range(2):
                    if s < 4 or (j % 2) == d:
                        sent(chunk(z, y, 0), zr_s.at[d, s - 1, j], zr_r.at[d, s - 1, j])

    @pl.when(c == 1)
    def _():
        step = (1, -1)
        send_chunk(own, ag_s.at[1], ag_r.at[1], dev(z, y, 1 - x, 1))
        for d in range(2):
            send_chunk(own, zr_s.at[d, 0, 0], zr_r.at[d, 0, 0], dev(z + step[d], y, x, 1))
        norm()

        def spread(k):
            zz = z + OFFS[k]
            for d in range(2):
                send_chunk(chunk(zz, y, 1), yr_s.at[d, 0, k], yr_r.at[d, 0, k], dev(z, y + step[d], x, 1))
            forward(zz, y, 1)

        other = shard(z, y, 1 - x, 1)
        got(other, ag_s.at[1], ag_r.at[1])
        for d in range(2):
            send_chunk(other, zr_s.at[d, 0, 1], zr_r.at[d, 0, 1], dev(z + step[d], y, x, 1))
        spread(0)
        for s in range(2, 5):
            for d in range(2):
                zz = z - step[d] * (s - 1)
                for j in range(2):
                    ref = shard(zz, y, (x + j) % 2, 1)
                    got(ref, zr_s.at[d, s - 2, j], zr_r.at[d, s - 2, j])
                    if s < 4 or j == d:
                        send_chunk(ref, zr_s.at[d, s - 1, j], zr_r.at[d, s - 1, j], dev(z + step[d], y, x, 1))
                spread(2 * (s - 1) - 1 + d)
            transpose(2 * s - 4, 2 * s - 2)
        for j in range(2):
            got(shard(z + 4, y, (x + j) % 2, 1), zr_s.at[j, 3, j], zr_r.at[j, 3, j])
        spread(7)
        for k in range(NZ):
            for d in range(2):
                ref = chunk(z + OFFS[k], y - step[d], 1)
                got(ref, yr_s.at[d, 0, k], yr_r.at[d, 0, k])
                if k % 2 == d:
                    send_chunk(ref, yr_s.at[d, 1, k], yr_r.at[d, 1, k], dev(z, y + step[d], x, 1))
                forward(z + OFFS[k], y - step[d], 1)
            if k == 3:
                transpose(6, 8)
        for k in range(NZ):
            d = k % 2
            got(chunk(z + OFFS[k], y + 2, 1), yr_s.at[d, 1, k], yr_r.at[d, 1, k])
            forward(z + OFFS[k], y + 2, 1)
        sent(own, ag_s.at[1], ag_r.at[1])
        for s in range(1, 5):
            for j in range(2):
                for d in range(2):
                    if s < 4 or j == d:
                        sent(own, zr_s.at[d, s - 1, j], zr_r.at[d, s - 1, j])
        for k in range(NZ):
            for d in range(2):
                sent(chunk(z, y, 1), yr_s.at[d, 0, k], yr_r.at[d, 0, k])
            sent(chunk(z, y, 1), yr_s.at[k % 2, 1, k], yr_r.at[k % 2, 1, k])

    def turned_copy():
        return copy(trans.at[:, :, :, 1 - c], trans_peer, tp_s, tp_r, partner)

    @pl.when(trainer)
    def _():
        turned_copy().start()
        position = (
            lax.broadcasted_iota(jnp.int32, owner_ref.shape, 0) * owner_ref.shape[1]
            + lax.broadcasted_iota(jnp.int32, owner_ref.shape, 1)
        )
        for q in range(3):
            for j in range(8):
                row = cand_s[q, j]
                owner = owner_s[row]
                same = (owner_ref[...] == owner) & (position < row)
                place_s[q * 8 + j] = owner * 3 + jnp.sum(same.astype(jnp.int32))

    def fw_got(k, carry):
        got(weight.at[k // NY, k % NY, :, 1 - c], fw_s.at[k], fw_r.at[k])
        return carry

    lax.fori_loop(0, NZ * NY, fw_got, 0)

    def hidden_step(n, carry):
        columns = pl.ds(pl.multiple_of(n * 256, 256), 256)
        block = weight[:, :, :, :, :, columns].reshape(width, 256)
        hidden = jnp.dot(normed[...], block, preferred_element_type=F32)
        act[:, columns] = jnp.tanh(hidden)
        return carry

    lax.fori_loop(0, emb // 256, hidden_step, 0)

    def fw_sent(k, carry):
        sent(weight.at[k // NY, k % NY, :, c], fw_s.at[k], fw_r.at[k])
        return carry

    lax.fori_loop(0, NZ * NY, fw_sent, 0)

    lanes = emb // 8
    length = tokens // 3
    places = lax.broadcasted_iota(jnp.int32, (length, lanes), 0)
    counts, masks = [], []
    for q in range(3):
        valid = (ids_ref[q : q + 1, :] != 0).astype(jnp.int32)
        count = jnp.sum(valid, axis=1, keepdims=True)
        counts.append(count.astype(F32))
        masks.append(places < count)
        for k in range(8):
            block = act[q * length : (q + 1) * length, k * lanes : (k + 1) * lanes]
            sums = jnp.sum(jnp.where(masks[q], block, 0.0), axis=0, keepdims=True)
            stage[q, k : k + 1, :] = sums / counts[q]

    def full_sum(v):
        return jnp.sum(jnp.sum(v, axis=1, keepdims=True), axis=0, keepdims=True)

    pooled, scales, units = [], [], []
    for q in range(3):
        pool = stage[q]
        scale = lax.rsqrt(full_sum(pool * pool) * (1.0 / emb) + 1e-06)
        pooled.append(pool)
        scales.append(scale)
        units.append(pool * scale)

    def e1(zz):
        return copy(stored, slab.at[z, y, x, c], e1_s.at[zz], e1_r.at[z], dev(zz, y, x, c, 0))

    @pl.when(g == 1)
    def _():
        for q in range(3):
            stored[q] = units[q].astype(BF)
        for zz in range(NZ):
            e1(zz).start()
        for zz in range(NZ):
            e1(zz).wait_send()
        weight_copy().wait_recv()
        out_ref[...] = wrecv[...].astype(F32)

    @pl.when(trainer)
    def _():
        weight_copy().wait_send()
        for zz in range(NZ):
            got(slab.at[zz, y, x, c], e1_s.at[zz], e1_r.at[zz])
        mine = slab.at[:, y, x, c]

        def e2(dy, dx):
            k = dy * 2 + dx
            return copy(mine, mine, e2_s.at[k], e2_r.at[k], dev(z, y + dy, (x + dx) % 2, c))

        def e3(yy, xx, k, cc):
            ref = slab.at[:, yy % NY, xx, cc]
            return copy(ref, ref, e3_s.at[k], e3_r.at[k], partner)

        rels = [(dy, dx) for dy in range(NY) for dx in range(2)]
        for dy, dx in rels:
            if dy or dx:
                e2(dy, dx).start()
        e3(y, x, 0, c).start()
        for dy, dx in rels:
            if dy or dx:
                k = dy * 2 + dx
                yy, xx = y - dy, (x + dx) % 2
                got(slab.at[:, yy % NY, xx, c], e2_s.at[k], e2_r.at[k])
                e3(yy, xx, k, c).start()
        for dy, dx in rels:
            k = dy * 2 + dx
            e3(y - dy, (x + dx) % 2, k, 1 - c).wait_recv()
        for q in range(3):
            rows, exps = [], []
            for j in range(8):
                p = place_s[q * 8 + j]
                o = p // 3
                row = slab[o // 16, (o // 4) % NY, (o // 2) % 2, o % 2, p - o * 3].astype(F32)
                rows.append(row)
                exps.append(jnp.exp(full_sum(units[q] * row) * (SHARPNESS / emb)))
            norm_sum = exps[0]
            for j in range(1, 8):
                norm_sum = norm_sum + exps[j]
            grad = jnp.zeros_like(rows[0])
            for j in range(8):
                weight_j = exps[j] / norm_sum - (1.0 if j == 0 else 0.0)
                grad = grad + weight_j * rows[j]
            grad = grad * (SHARPNESS / emb)
            inner = full_sum(pooled[q] * grad)
            scale = scales[q]
            stage[q] = scale * grad - pooled[q] * (scale * scale * scale) * inner * (1.0 / emb)
        dl = []
        for q in range(3):
            span = slice(q * length, (q + 1) * length)
            for k in range(8):
                cols = slice(k * lanes, (k + 1) * lanes)
                a = act[span, cols]
                base = jnp.where(masks[q], 1.0 / counts[q], 0.0) * stage[q, k : k + 1, :]
                delta[span, cols] = (base * (1.0 - a * a)).astype(BF)
            dl.append(copy(delta.at[span], delta_peer.at[span], dl_s.at[q], dl_r.at[q], partner))
            if q > 0:
                dl[q - 1].start()
        dl[2].start()
        for dy, dx in rels:
            k = dy * 2 + dx
            if k:
                e2(dy, dx).wait_send()
            e3(y - dy, (x + dx) % 2, k, c).wait_send()
        turned_copy().wait_recv()
        for q in range(3):
            dl[q].wait_recv()

        def piece_at(k):
            return piece_s.at[k]

        def unit(u, lhs, lhs_peer):
            value = jnp.dot(lhs.reshape(256, tokens), delta[...], preferred_element_type=F32)
            value = value + jnp.dot(lhs_peer.reshape(256, tokens), delta_peer[...], preferred_element_type=F32)
            part[u] = value.reshape(4, 64, emb)

        def finish(value):
            mean_square = jnp.sum(value * value, axis=1, keepdims=True) * (1.0 / emb)
            out_ref[...] = value * lax.rsqrt(mean_square + 1e-06)

        step = (1, -1)

        @pl.when(c == 0)
        def _():
            def compute(i, carry):
                u = (z + 4 + i) % NZ
                unit(u, trans[u, :, :, 0], trans_peer[u])
                return carry

            def ring(d, s, j):
                k = (s - 1) * 4 + j
                return copy(
                    big_s.at[d, k], big_r.at[d, k], bg_ss.at[d, k], bg_rs.at[d, k],
                    dev(z + step[d], y, x, 0),
                )

            compute(0, 0)
            for j in range(4):
                d = j % 2
                big_s[d, j] = part[(z + 4) % NZ, j].astype(BF)
            for j in range(4):
                ring(j % 2, 1, j).start()
            lax.fori_loop(1, NZ, compute, 0)
            for s in range(2, 5):
                for j in (range(4) if s > 2 else (0, 1, 2, 3)):
                    for d in range(2):
                        k = (s - 1) * 4 + j
                        value = part[(z + step[d] * (5 - s)) % NZ, j]
                        if s > 2 or j % 2 == d:
                            ring(d, s - 1, j).wait_recv()
                            value = value + big_r[d, k - 4].astype(F32)
                        big_s[d, k] = value.astype(BF)
                        ring(d, s, j).start()
            for j in range(4):
                value = part[z, j]
                for d in range(2):
                    ring(d, 4, j).wait_recv()
                    value = value + big_r[d, 12 + j].astype(F32)
                total[j] = value.reshape(2, 32, emb)
                piece_s[2 * j : 2 * j + 2] = value.astype(BF).reshape(2, 32, emb)

            def swap(dy, dx):
                k = dy * 2 + dx
                yy, xx = (y + dy) % NY, (x + dx) % 2
                return copy(
                    piece_s.at[yy * 2 + xx], piece_r.at[k], pc_ss.at[k], pc_rs.at[k], dev(z, yy, xx, 0)
                )

            for dy, dx in rels:
                if dy or dx:
                    swap(dy, dx).start()
            value = total[y, x]
            for dy, dx in rels:
                if dy or dx:
                    swap(dy, dx).wait_recv()
                    value = value + piece_r[dy * 2 + dx].astype(F32)
            finish(value)
            for dy, dx in rels:
                if dy or dx:
                    swap(dy, dx).wait_send()
            for s in range(1, 5):
                for j in range(4):
                    for d in range(2):
                        if s > 1 or j % 2 == d:
                            ring(d, s, j).wait_send()

        @pl.when(c == 1)
        def _():
            def compute(i, carry):
                yy = (y + 2 + i // 2) % NY
                h = i % 2
                half = pl.ds(h * 4, 4)
                unit(yy * 2 + h, trans[half, yy, :, 1], trans_peer[half, yy])
                return carry

            def local(yy, j):
                zz = (z + RS_OFFS[j]) % NZ
                return part[(yy % NY) * 2 + zz // 4, zz % 4]

            def ring(d, s, j):
                k = (s - 1) * 8 + j
                return copy(
                    big_s.at[d, k], big_r.at[d, k], bg_ss.at[d, k], bg_rs.at[d, k],
                    dev(z, y + step[d], x, 1),
                )

            lax.fori_loop(0, 2, compute, 0)
            for j in range(8):
                big_s[j % 2, j] = local(y + 2, j).astype(BF)
            for j in range(8):
                ring(j % 2, 1, j).start()
            lax.fori_loop(2, NZ, compute, 0)
            for j in range(8):
                for d in range(2):
                    value = local(y + step[d], j)
                    if j % 2 == d:
                        ring(d, 1, j).wait_recv()
                        value = value + big_r[d, j].astype(F32)
                    big_s[d, 8 + j] = value.astype(BF)
                    ring(d, 2, j).start()

            def landed(j):
                value = local(y, j)
                for d in range(2):
                    ring(d, 2, j).wait_recv()
                    value = value + big_r[d, 8 + j].astype(F32)
                return value.reshape(2, 32, emb)

            def ring2(d, s, j):
                k = (s - 1) * 2 + j
                return copy(
                    small_s.at[d, k], small_r.at[d, k], sm_ss.at[d, k], sm_rs.at[d, k],
                    dev(z + step[d], y, x, 1),
                )

            value = landed(0)
            for j in range(2):
                small_s[j, j] = value[j].astype(BF)
            for j in range(2):
                ring2(j, 1, j).start()
            for s in range(2, 5):
                for d in range(2):
                    value = landed(2 * s - 3 + d)
                    for j in range(2):
                        k = (s - 1) * 2 + j
                        v = value[j]
                        if s > 2 or j == d:
                            ring2(d, s - 1, j).wait_recv()
                            v = v + small_r[d, k - 2].astype(F32)
                        small_s[d, k] = v.astype(BF)
                        ring2(d, s, j).start()
            value = landed(7)
            for j in range(2):
                v = value[j]
                for d in range(2):
                    ring2(d, 4, j).wait_recv()
                    v = v + small_r[d, 6 + j].astype(F32)
                total[0, j] = v
                piece_s[j] = v.astype(BF)
            last = copy(piece_s.at[1 - x], piece_r.at[1], pc_ss.at[1], pc_rs.at[1], dev(z, y, 1 - x, 1))
            last.start()
            last.wait_recv()
            finish(total[0, x] + piece_r[1].astype(F32))
            last.wait_send()
            for j in range(8):
                ring(j % 2, 1, j).wait_send()
                for d in range(2):
                    ring(d, 2, j).wait_send()
            for s in range(1, 5):
                for j in range(2):
                    for d in range(2):
                        if s > 1 or j == d:
                            ring2(d, s, j).wait_send()

        turned_copy().wait_send()
        for q in range(3):
            dl[q].wait_send()


def shards(token_states, token_ids, master, gain, cand_ids, slab_owner):
    seqs, length, width = token_states.shape[1:]
    tokens = seqs * length
    rows, emb = master.shape[1:]
    vmem = pl.BlockSpec(memory_space=pltpu.VMEM)
    smem = pl.BlockSpec(memory_space=pltpu.SMEM)
    dma = pltpu.SemaphoreType.DMA
    V = pltpu.VMEM
    out = pl.pallas_call(
        body,
        out_shape=jax.ShapeDtypeStruct((rows, emb), F32),
        in_specs=[pl.BlockSpec(memory_space=pl.ANY), vmem, vmem, vmem, vmem, smem, smem],
        out_specs=vmem,
        scratch_shapes=[
            V((tokens, width), BF),
            V((tokens, width), BF),
            V((NZ, NY, 2, 2, rows, tokens), BF),
            V((NZ, NY, 2, rows, tokens), BF),
            V((NZ, NY, 2, 2, rows, emb), BF),
            V((rows, emb), BF),
            V((tokens, emb), F32),
            V((3, 8, emb // 8), F32),
            V((3, 8, emb // 8), BF),
            V((NZ, NY, 2, 2, 3, 8, emb // 8), BF),
            V((tokens, emb), BF),
            V((tokens, emb), BF),
            V((NZ, 4, 64, emb), F32),
            V((4, 2, rows, emb), F32),
            V((2, 16, 64, emb), BF),
            V((2, 16, 64, emb), BF),
            V((2, 8, rows, emb), BF),
            V((2, 8, rows, emb), BF),
            V((8, rows, emb), BF),
            V((8, rows, emb), BF),
            pltpu.SMEM((24,), jnp.int32),
            dma,
            dma((8,)), dma((8,)),
            dma((2, 4, 4)), dma((2, 4, 4)),
            dma((2, 2, 8)), dma((2, 2, 8)),
            dma((32,)), dma((32,)),
            dma, dma,
            dma, dma,
            dma((8,)), dma((8,)),
            dma((8,)), dma((8,)),
            dma((8,)), dma((8,)),
            dma((3,)), dma((3,)),
            dma((2, 16)), dma((2, 16)),
            dma((2, 8)), dma((2, 8)),
            dma((8,)), dma((8,)),
        ],
        compiler_params=pltpu.CompilerParams(
            collective_id=0, has_side_effects=True, vmem_limit_bytes=62 * 1024 * 1024
        ),
    )(
        token_states.reshape(tokens, width),
        token_ids[0],
        master[0],
        gain.reshape(1, width),
        slab_owner.reshape(3, -1),
        cand_ids,
        slab_owner,
    )
    return out[None]


def solution(mesh):
    placed = (
        P("grp", "fsdp", None, None),
        P("grp", "fsdp", None),
        P("grp", "fsdp", None),
        P(),
        P("fsdp", None),
        P(),
    )
    return jax.shard_map(
        shards, mesh=mesh, in_specs=placed, out_specs=P("grp", "fsdp", None), check_vma=False
    )
```

time: 1050 us -> 107 us (0.10); the launches traced: 1040 us -> 107 us
  waiting for transfers between devices: 819 us -> 0 us
  blocking collectives: 164 us -> 0 us
  Pallas kernels: 0 us -> 104 us
  matrix products: 15.4 us -> 0 us
  between operations: 13.5 us -> 0.01 us
  other arithmetic: 13.1 us -> 0 us
    reduce_scatter x1 -> x0, waiting for transfers between devices: 583 us -> none  [shards(): lax.psum_scatter(lax.cond(trainer, compute, lambda: jnp.zeros((lax.axis_s...]
    all_gather x1 -> x0, waiting for transfers between devices: 213 us -> none  [shards(): lax.all_gather(weight_bf, 'fsdp', axis=0, tiled=True)]
    all_gather x1 -> x0, blocking collectives: 164 us -> none  [shards(): whole = lax.all_gather(stored, 'fsdp', axis=0, tiled=True)]
    pallas_call x0 -> x1, Pallas kernels: none -> 104 us  [shards(): pl.pallas_call(body, out_shape=jax.ShapeDtypeStruct((rows, emb), F32), in...]
    ppermute x2 -> x0, waiting for transfers between devices: 22 us -> none  [passed_along(): return lax.ppermute(shard, axis, pairs)]
    dot_general x4 -> x0, matrix products: 15.4 us -> none  [the longest x1 9.23 us: compute(): lax.dot_general(normed, delta, (((0,), (0,)), ((), ())), preferred_elemen...]
  transfers between devices with their start and end apart: 4 -> 0, of which waited for: 3 -> 0; matrix products, arithmetic and copies ran while one was open for 1% -> 0% of each run, Pallas kernels for 0% -> 0%
where the time goes in v1:
time: 107 us
  Pallas kernels  104 us (97%)
  local copies, waits for them, and re-layouts  2.83 us (3%)
    pallas_call x1, Pallas kernels, shards(): pl.pallas_call(body, out_shape=jax.ShapeDtypeStruct((rows, emb), F32), in...  104 us
    unnamed x2, local copies, waits for them, and re-layouts  2.83 us

profile of v1, /device:TPU:8, one launch (start us, length us, event | category | flops | bytes accessed | tf_op | source)
XLA Modules:
  0.0 106.8 jit_solution(11785563306082899933)
XLA Ops:
  0.0 1.3 %copy.9 = s32[1,3,128]{2,1,0:T(4,128)} copy(s32[1,3,128]{2,0,1:T(1,128)} %param.7) | data formatting | bytes 3072
  1.3 103.9 %shard_map.64 = f32[32,1024]{1,0:T(8,128)} custom-call(bf16[384,4096]{1,0:T(8,128)(2,1)} %bitcast.8, s32[3,128]{1,0:T(4,128)} %bitcast.12, f32[32,1024]{1,0:T(8,128)} %bitcast.10, f32[1,4096]{1,0:T(1,128)} %bitcast.11, s32[3,128]{1,0:T(4,128)} %bitcast.13, s32[3,8]{1,0:T(4,128)} %cand_s.1, s32[384]{0:T(512)} %owner_s.1), custom_call_target="tpu_custom_call" | custom-call | tf_op jit(solution)/shard_map/pallas_call | solution.py:537
  105.2 1.6 %copy.11 = f32[1,32,1024]{2,1,0:T(8,128)} copy(f32[1,32,1024]{2,1,0:T(8,128)} %bitcast.9) | data formatting | bytes 262144

commit v2 on v1

v2 whole, which is shorter than its diff:
```python
import jax
import jax.numpy as jnp
from jax import lax
from jax.experimental import pallas as pl
from jax.experimental.pallas import tpu as pltpu
from jax.sharding import PartitionSpec as P

MESH = pl.DeviceIdType.MESH
SHARPNESS = 20.0
NZ, NY = 8, 4
BF, F32 = jnp.bfloat16, jnp.float32
OFFS = (0, -1, 1, -2, 2, -3, 3, 4)
RS_OFFS = (4, 3, -3, 2, -2, 1, -1, 0)
J_ORDER = (0, 1, 3, 2)
AG_XL = (1, 3, 2)
RS_XL = (1, 3, 2)
STEP = (1, -1)
NEAR = (0, 1, -1, 2, -2)
FAR = (3, -3, 4)


def units_of(x_last):
    pairs = []
    for j in J_ORDER:
        pairs.append((j, 0))
        if j not in x_last:
            pairs.append((j, 1))
    return pairs


def body(
    states_hbm, master_hbm, gain_hbm, ids_ref, owner_ref, cand_s, owner_s, out_ref,
    states, master, gain, normed, trans, trans_peer, weight, wrecv, act, stage, stored, slab,
    delta, delta_peer, part, total, big_s, big_r, x1_s, x1_r, small_s, small_r, fin_s, fin_r, place_s,
    ld_sem, ay_s, ay_r, xf_s, xf_r, zr_s, zr_r, yr_s, yr_r, fw_s, fw_r, wt_s, wt_r, tp_s, tp_r,
    e1_s, e1_r, e2_s, e2_r, e3_s, e3_r, dl_s, dl_r, bg_ss, bg_rs, xx_ss, xx_rs, sm_ss, sm_rs, fi_ss, fi_rs,
):
    g = lax.axis_index("grp")
    f = lax.axis_index("fsdp")
    c = f % 2
    x = (f // 2) % 2
    y = (f // 4) % NY
    z = f // 16
    tokens, width = states.shape
    emb = weight.shape[-1]

    def dev(zz, yy, xx, cc, gg=None):
        index = (((zz % NZ) * NY + yy % NY) * 2 + xx) * 2 + cc
        return (g if gg is None else gg, index)

    def copy(src, dst, ssem, rsem, to):
        return pltpu.make_async_remote_copy(
            src_ref=src, dst_ref=dst, send_sem=ssem, recv_sem=rsem,
            device_id=to, device_id_type=MESH,
        )

    me = (g, f)
    partner = dev(z, y, x, 1 - c)
    x_next = dev(z, y, 1 - x, c)
    trainer = g == 0

    load_master = pltpu.make_async_copy(master_hbm, master, ld_sem.at[0])
    load_gain = pltpu.make_async_copy(gain_hbm, gain, ld_sem.at[1])
    load = pltpu.make_async_copy(states_hbm, states, ld_sem.at[2])
    load_master.start()
    load_gain.start()
    load.start()

    barrier = pltpu.get_barrier_semaphore()
    peers = [dev(z, y + 1, x, c), dev(z, y + 2, x, c), dev(z, y + 3, x, c)]
    peers += [dev(z + 1, y, x, c), dev(z - 1, y, x, c), x_next, partner, (1 - g, f)]
    for peer in peers:
        pl.semaphore_signal(barrier, inc=1, device_id=peer, device_id_type=MESH)
    load_master.wait()
    weight[z, y, x, c] = master[...].astype(BF)
    pl.semaphore_wait(barrier, len(peers))

    def shard(zz, yy, xx, cc):
        return weight.at[zz % NZ, yy % NY, xx % 2, cc]

    def push(ref, ssem, rsem, to):
        copy(ref, ref, ssem, rsem, to).start()

    def got(ref, ssem, rsem):
        copy(ref, ref, ssem, rsem, me).wait_recv()

    def sent(ref, ssem, rsem):
        copy(ref, ref, ssem, rsem, me).wait_send()

    def forward(zz, yy, xx, cc):
        k = ((zz % NZ) * NY + yy % NY) * 2 + xx % 2
        push(shard(zz, yy, xx, cc), fw_s.at[k], fw_r.at[k], partner)

    own = shard(z, y, x, c)

    def norm_step(i, carry):
        rows = pl.ds(pl.multiple_of(i * 16, 16), 16)
        wide = states[rows, :].astype(F32)
        mean_square = jnp.sum(wide * wide, axis=-1, keepdims=True) * (1.0 / width)
        normed[rows, :] = (wide * lax.rsqrt(mean_square + 1e-05) * gain[...]).astype(BF)
        return carry

    def norm():
        load_gain.wait()
        load.wait()
        lax.fori_loop(0, tokens // 16, norm_step, 0)

    def transpose_step(i, carry):
        columns = pl.ds(pl.multiple_of(i * 512, 512), 512)
        turned = jnp.transpose(normed[:, columns])
        trans[i] = turned.reshape(NY, 2, 2, 32, tokens)
        return carry

    def transpose(lo, hi):
        lax.fori_loop(lo, hi, transpose_step, 0)

    def weight_copy():
        return copy(own, wrecv, wt_s, wt_r, (1 - g, f))

    def weight_start():
        @pl.when(trainer)
        def _():
            weight_copy().start()

    @pl.when(c == 0)
    def _():
        units = units_of(AG_XL)

        def ring(zz, u, s, d):
            j, i = units[u]
            push(
                shard(zz, y + j, x + i, 0), zr_s.at[d, s - 1, u], zr_r.at[d, s - 1, u],
                dev(z + STEP[d], y, x, 0),
            )

        def cross(zz, j):
            k = (zz % NZ) * NY + j
            push(shard(zz, y + j, x, 0), xf_s.at[k], xf_r.at[k], x_next)

        def crossed(zz, j):
            k = (zz % NZ) * NY + j
            got(shard(zz, y + j, x + 1, 0), xf_s.at[k], xf_r.at[k])
            forward(zz, y + j, x + 1, 0)

        for d in range(2):
            ring(z, 0, 1, d)
        cross(z, 0)
        for j in (1, 3, 2):
            push(own, ay_s.at[j], ay_r.at[j], dev(z, y + j, x, 0))
        forward(z, y, x, 0)
        norm()
        crossed(z, 0)
        for d in range(2):
            ring(z, units.index((0, 1)), 1, d)
        for j in (1, 3, 2):
            got(shard(z, y + j, x, 0), ay_s.at[(-j) % NY], ay_r.at[(-j) % NY])
            for d in range(2):
                ring(z, units.index((j, 0)), 1, d)
            cross(z, j)
            forward(z, y + j, x, 0)
        for j in (1, 3, 2):
            if j not in AG_XL:
                crossed(z, j)
                for d in range(2):
                    ring(z, units.index((j, 1)), 1, d)
        transpose(0, 2)

        def serve(zz, first):
            for j in AG_XL:
                crossed(zz, j)

        for s in range(2, 5):
            for u, (j, i) in enumerate(units):
                for d in range(2):
                    zz = z - STEP[d] * (s - 1)
                    got(shard(zz, y + j, x + i, 0), zr_s.at[d, s - 2, u], zr_r.at[d, s - 2, u])
                    if s < 4 or u % 2 == d:
                        ring(zz, u, s, d)
                    if j in AG_XL:
                        cross(zz, j)
                    forward(zz, y + j, x + i, 0)
            if s == 2:
                serve(z, True)
            else:
                for d in range(2):
                    serve(z - STEP[d] * (s - 2), False)
            transpose(2 * s - 2, 2 * s)
        for u, (j, i) in enumerate(units):
            d = u % 2
            got(shard(z + 4, y + j, x + i, 0), zr_s.at[d, 3, u], zr_r.at[d, 3, u])
            if j in AG_XL:
                cross(z + 4, j)
            forward(z + 4, y + j, x + i, 0)
        weight_start()
        for zz in (z - 3, z + 3, z + 4):
            serve(zz, False)
        for j in (1, 3, 2):
            sent(own, ay_s.at[j], ay_r.at[j])
        for u in range(len(units)):
            for s in range(1, 5):
                for d in range(2):
                    if s < 4 or u % 2 == d:
                        sent(own, zr_s.at[d, s - 1, u], zr_r.at[d, s - 1, u])
        for off in range(NZ):
            for j in range(NY):
                if j in AG_XL or off == 0:
                    k = ((z + off) % NZ) * NY + j
                    sent(own, xf_s.at[k], xf_r.at[k])

    @pl.when(c == 1)
    def _():
        def ring(zz, i, s, d):
            push(
                shard(zz, y, x + i, 1), zr_s.at[d, s - 1, i], zr_r.at[d, s - 1, i],
                dev(z + STEP[d], y, x, 1),
            )

        def spread(k, i):
            ref = shard(z + OFFS[k], y, x + i, 1)
            for d in range(2):
                push(ref, yr_s.at[d, 0, 2 * k + i], yr_r.at[d, 0, 2 * k + i], dev(z, y + STEP[d], x, 1))
            forward(z + OFFS[k], y, x + i, 1)

        def serve(k):
            for i in range(2):
                for d in range(2):
                    yy = y - STEP[d]
                    ref = shard(z + OFFS[k], yy, x + i, 1)
                    got(ref, yr_s.at[d, 0, 2 * k + i], yr_r.at[d, 0, 2 * k + i])
                    if i == d:
                        push(ref, yr_s.at[d, 1, k], yr_r.at[d, 1, k], dev(z, y + STEP[d], x, 1))
                    forward(z + OFFS[k], yy, x + i, 1)

        push(own, ay_s.at[0], ay_r.at[0], x_next)
        for d in range(2):
            ring(z, 0, 1, d)
        spread(0, 0)
        norm()
        got(shard(z, y, x + 1, 1), ay_s.at[0], ay_r.at[0])
        for d in range(2):
            ring(z, 1, 1, d)
        spread(0, 1)
        transpose(0, 1)
        for s in range(2, 5):
            for d in range(2):
                zz = z - STEP[d] * (s - 1)
                for i in range(2):
                    got(shard(zz, y, x + i, 1), zr_s.at[d, s - 2, i], zr_r.at[d, s - 2, i])
                    if s < 4 or i == d:
                        ring(zz, i, s, d)
                    spread(2 * s - 3 + d, i)
            for k in (0,) if s == 2 else (2 * s - 5, 2 * s - 4):
                serve(k)
            transpose(2 * s - 3, 2 * s - 1)
        for i in range(2):
            got(shard(z + 4, y, x + i, 1), zr_s.at[i, 3, i], zr_r.at[i, 3, i])
            spread(7, i)
        weight_start()
        transpose(7, 8)
        for k in (5, 6, 7):
            serve(k)
        for k in range(NZ):
            for d in range(2):
                got(shard(z + OFFS[k], y + 2, x + d, 1), yr_s.at[d, 1, k], yr_r.at[d, 1, k])
                forward(z + OFFS[k], y + 2, x + d, 1)
        sent(own, ay_s.at[0], ay_r.at[0])
        for s in range(1, 5):
            for i in range(2):
                for d in range(2):
                    if s < 4 or i == d:
                        sent(own, zr_s.at[d, s - 1, i], zr_r.at[d, s - 1, i])
        for k in range(NZ):
            for d in range(2):
                for i in range(2):
                    sent(own, yr_s.at[d, 0, 2 * k + i], yr_r.at[d, 0, 2 * k + i])
                sent(own, yr_s.at[d, 1, k], yr_r.at[d, 1, k])

    def turned_copy():
        return copy(trans.at[:, :, :, 1 - c], trans_peer, tp_s, tp_r, partner)

    @pl.when(trainer)
    def _():
        turned_copy().start()
        position = (
            lax.broadcasted_iota(jnp.int32, owner_ref.shape, 0) * owner_ref.shape[1]
            + lax.broadcasted_iota(jnp.int32, owner_ref.shape, 1)
        )
        for q in range(3):
            for j in range(8):
                row = cand_s[q, j]
                owner = owner_s[row]
                same = (owner_ref[...] == owner) & (position < row)
                place_s[q * 8 + j] = owner * 3 + jnp.sum(same.astype(jnp.int32))

    def fw_got(k, carry):
        got(weight.at[k // 8, (k // 2) % NY, k % 2, 1 - c], fw_s.at[k], fw_r.at[k])
        return carry

    lax.fori_loop(0, 64, fw_got, 0)

    def hidden_step(n, carry):
        columns = pl.ds(pl.multiple_of(n * 256, 256), 256)
        block = weight[:, :, :, :, :, columns].reshape(width, 256)
        hidden = jnp.dot(normed[...], block, preferred_element_type=F32)
        act[:, columns] = jnp.tanh(hidden)
        return carry

    lax.fori_loop(0, emb // 256, hidden_step, 0)

    def fw_sent(k, carry):
        sent(weight.at[k // 8, (k // 2) % NY, k % 2, c], fw_s.at[k], fw_r.at[k])
        return carry

    lax.fori_loop(0, 64, fw_sent, 0)

    lanes = emb // 8
    length = tokens // 3
    places = lax.broadcasted_iota(jnp.int32, (length, lanes), 0)
    counts, masks = [], []
    for q in range(3):
        valid = (ids_ref[q] != 0).astype(jnp.int32)
        count = jnp.sum(valid, axis=1, keepdims=True)
        counts.append(count.astype(F32))
        masks.append(places < count)
        for k in range(8):
            block = act[q * length : (q + 1) * length, k * lanes : (k + 1) * lanes]
            sums = jnp.sum(jnp.where(masks[q], block, 0.0), axis=0, keepdims=True)
            stage[q, k : k + 1, :] = sums / counts[q]

    def full_sum(v):
        return jnp.sum(jnp.sum(v, axis=1, keepdims=True), axis=0, keepdims=True)

    pooled, scales, units = [], [], []
    for q in range(3):
        pool = stage[q]
        scale = lax.rsqrt(full_sum(pool * pool) * (1.0 / emb) + 1e-06)
        pooled.append(pool)
        scales.append(scale)
        units.append(pool * scale)

    def e1(zz):
        return copy(stored, slab.at[z, y, x, c], e1_s.at[zz % NZ], e1_r.at[z], dev(zz, y, x, c, 0))

    @pl.when(g == 1)
    def _():
        for q in range(3):
            stored[q] = units[q].astype(BF)
        weight_copy().wait_recv()
        for off in (4, 3, -3, 2, -2, 1, -1, 0):
            e1(z + off).start()
        out_ref[...] = wrecv[...].astype(F32)
        for zz in range(NZ):
            e1(zz).wait_send()

    @pl.when(trainer)
    def _():
        rels = [(dy, dx) for dy in range(NY) for dx in range(2)]
        sends = [(2, 0), (2, 1), (1, 0), (3, 0), (1, 1), (3, 1), (0, 1)]

        def e2(b, dy, dx):
            k = b * 8 + dy * 2 + dx
            to = dev(z, y + dy, (x + dx) % 2, c)
            for off in (NEAR, FAR)[b]:
                ref = slab.at[(z + off) % NZ, y, x, c]
                push(ref, e2_s.at[k], e2_r.at[k], to)

        def e3(yy, xx, k, cc):
            ref = slab.at[:, yy % NY, xx, cc]
            return copy(ref, ref, e3_s.at[k], e3_r.at[k], partner)

        for b in range(2):
            for off in (NEAR, FAR)[b]:
                zz = (z + off) % NZ
                got(slab.at[zz, y, x, c], e1_s.at[zz], e1_r.at[zz])
            for dy, dx in sends:
                e2(b, dy, dx)
        e3(y, x, 0, c).start()
        for dy, dx in ((0, 1), (1, 0), (3, 0), (1, 1), (3, 1), (2, 0), (2, 1)):
            k = dy * 2 + dx
            yy, xx = (y - dy) % NY, (x + dx) % 2
            got(slab.at[0:5, yy, xx, c], e2_s.at[k], e2_r.at[k])
            got(slab.at[0:3, yy, xx, c], e2_s.at[8 + k], e2_r.at[8 + k])
            e3(yy, xx, k, c).start()
        for dy, dx in rels:
            k = dy * 2 + dx
            e3(y - dy, (x + dx) % 2, k, 1 - c).wait_recv()
        for q in range(3):
            rows, exps = [], []
            for j in range(8):
                p = place_s[q * 8 + j]
                o = p // 3
                row = slab[o // 16, (o // 4) % NY, (o // 2) % 2, o % 2, p - o * 3].astype(F32)
                rows.append(row)
                exps.append(jnp.exp(full_sum(units[q] * row) * (SHARPNESS / emb)))
            norm_sum = exps[0]
            for j in range(1, 8):
                norm_sum = norm_sum + exps[j]
            grad = jnp.zeros_like(rows[0])
            for j in range(8):
                weight_j = exps[j] / norm_sum - (1.0 if j == 0 else 0.0)
                grad = grad + weight_j * rows[j]
            grad = grad * (SHARPNESS / emb)
            inner = full_sum(pooled[q] * grad)
            scale = scales[q]
            stage[q] = scale * grad - pooled[q] * (scale * scale * scale) * inner * (1.0 / emb)
        dl = []
        for q in range(3):
            span = slice(q * length, (q + 1) * length)
            for k in range(8):
                cols = slice(k * lanes, (k + 1) * lanes)
                a = act[span, cols]
                base = jnp.where(masks[q], 1.0 / counts[q], 0.0) * stage[q, k : k + 1, :]
                delta[span, cols] = (base * (1.0 - a * a)).astype(BF)
            dl.append(copy(delta.at[span], delta_peer.at[span], dl_s.at[q], dl_r.at[q], partner))
            if q > 0:
                dl[q - 1].start()
        dl[2].start()
        for dy, dx in rels:
            k = dy * 2 + dx
            if k:
                sent(slab.at[0:5, y, x, c], e2_s.at[k], e2_r.at[k])
                sent(slab.at[0:3, y, x, c], e2_s.at[8 + k], e2_r.at[8 + k])
            e3(y - dy, (x + dx) % 2, k, c).wait_send()
        weight_copy().wait_send()
        turned_copy().wait_recv()
        for q in range(3):
            dl[q].wait_recv()

        def unit(u, lhs, lhs_peer):
            value = jnp.dot(lhs.reshape(256, tokens), delta[...], preferred_element_type=F32)
            value = value + jnp.dot(lhs_peer.reshape(256, tokens), delta_peer[...], preferred_element_type=F32)
            part[u] = value.reshape(8, 32, emb)

        def finish(value):
            mean_square = jnp.sum(value * value, axis=1, keepdims=True) * (1.0 / emb)
            out_ref[...] = value * lax.rsqrt(mean_square + 1e-06)

        @pl.when(c == 0)
        def _():
            pairs = units_of(RS_XL)
            count = len(pairs)

            def slot(j, i):
                return ((y + j) % NY) * 2 + (x + i) % 2

            def x_first(b, n):
                k = b * 3 + n
                return copy(x1_s.at[k], x1_r.at[k], xx_ss.at[k], xx_rs.at[k], x_next)

            def compute(b, carry):
                odd = b % 2
                off = odd * ((7 - b) // 2) - (1 - odd) * ((8 - b) // 2)
                zz = (z + 16 + off) % NZ
                unit(zz, trans[zz, :, :, 0], trans_peer[zz])
                for n, j in enumerate(RS_XL):
                    x1_s[b * 3 + n] = part[zz, slot(j, 1)].astype(BF)
                return carry

            def compute_send(b, carry):
                compute(b, carry)
                for n in range(len(RS_XL)):
                    x_first(b, n).start()
                return carry

            def ring(d, s, u):
                k = (s - 1) * count + u
                return copy(
                    big_s.at[d, k], big_r.at[d, k], bg_ss.at[d, k], bg_rs.at[d, k],
                    dev(z + STEP[d], y, x, 0),
                )

            def local(b, u):
                j, i = pairs[u]
                value = part[(z + RS_OFFS[b]) % NZ, slot(j, i)]
                if j in RS_XL:
                    n = RS_XL.index(j)
                    x_first(b, n).wait_recv()
                    value = value + x1_r[b * 3 + n].astype(F32)
                return value

            def first(u):
                d = u % 2
                big_s[d, u] = local(0, u).astype(BF)
                ring(d, 1, u).start()

            plain = [u for u, (j, i) in enumerate(pairs) if j not in RS_XL]
            compute_send(0, 0)
            for u in plain:
                first(u)
            lax.fori_loop(1, 4, compute_send, 0)
            for u in range(count):
                if u not in plain:
                    first(u)
            lax.fori_loop(4, NZ, compute_send, 0)
            for s in range(2, 5):
                for u in range(count):
                    for d in range(2):
                        k = (s - 1) * count + u
                        value = local(2 * s - 3 + d, u)
                        if s > 2 or u % 2 == d:
                            ring(d, s - 1, u).wait_recv()
                            value = value + big_r[d, k - count].astype(F32)
                        big_s[d, k] = value.astype(BF)
                        ring(d, s, u).start()

            def last(j, i):
                k = j * 2 + i
                return copy(
                    fin_s.at[k], fin_r.at[k], fi_ss.at[k], fi_rs.at[k], dev(z, y + j, (x + i) % 2, 0)
                )

            for u in list(range(1, count)) + [0]:
                j, i = pairs[u]
                value = local(7, u)
                for d in range(2):
                    ring(d, 4, u).wait_recv()
                    value = value + big_r[d, 3 * count + u].astype(F32)
                if u:
                    fin_s[j * 2 + i] = value.astype(BF)
                    last(j, i).start()
                else:
                    total[0] = value
            value = total[0]
            for j, i in pairs[1:]:
                last(j, i).wait_recv()
                value = value + fin_r[j * 2 + i].astype(F32)
            finish(value)
            for j, i in pairs[1:]:
                last(j, i).wait_send()
            for b in range(NZ):
                for n in range(len(RS_XL)):
                    x_first(b, n).wait_send()
            for s in range(1, 5):
                for u in range(count):
                    for d in range(2):
                        if s > 1 or u % 2 == d:
                            ring(d, s, u).wait_send()

        @pl.when(c == 1)
        def _():
            def compute(i, carry):
                yy = (y + 2 + i // 2) % NY
                h = i % 2
                half = pl.ds(h * 4, 4)
                unit(yy * 2 + h, trans[half, yy, :, 1], trans_peer[half, yy])
                return carry

            def local(yy, j):
                zz = (z + RS_OFFS[j]) % NZ
                return part[(yy % NY) * 2 + zz // 4, pl.ds((zz % 4) * 2, 2)]

            def ring(d, s, j):
                k = (s - 1) * 8 + j
                span = pl.ds(2 * k, 2)
                return copy(
                    big_s.at[d, span], big_r.at[d, span], bg_ss.at[d, k], bg_rs.at[d, k],
                    dev(z, y + STEP[d], x, 1),
                )

            lax.fori_loop(0, 2, compute, 0)
            for j in range(8):
                big_s[j % 2, 2 * j : 2 * j + 2] = local(y + 2, j).astype(BF)
                ring(j % 2, 1, j).start()
            lax.fori_loop(2, NZ, compute, 0)
            for j in range(8):
                for d in range(2):
                    value = local(y + STEP[d], j)
                    if j % 2 == d:
                        ring(d, 1, j).wait_recv()
                        value = value + big_r[d, 2 * j : 2 * j + 2].astype(F32)
                    big_s[d, 16 + 2 * j : 18 + 2 * j] = value.astype(BF)
                    ring(d, 2, j).start()

            def landed(j):
                value = local(y, j)
                for d in range(2):
                    ring(d, 2, j).wait_recv()
                    value = value + big_r[d, 16 + 2 * j : 18 + 2 * j].astype(F32)
                return value

            def ring2(d, s, j):
                k = (s - 1) * 2 + j
                return copy(
                    small_s.at[d, k], small_r.at[d, k], sm_ss.at[d, k], sm_rs.at[d, k],
                    dev(z + STEP[d], y, x, 1),
                )

            value = landed(0)
            for j in range(2):
                small_s[j, j] = value[j].astype(BF)
            for j in range(2):
                ring2(j, 1, j).start()
            for s in range(2, 5):
                for d in range(2):
                    value = landed(2 * s - 3 + d)
                    for j in range(2):
                        k = (s - 1) * 2 + j
                        v = value[j]
                        if s > 2 or j == d:
                            ring2(d, s - 1, j).wait_recv()
                            v = v + small_r[d, k - 2].astype(F32)
                        small_s[d, k] = v.astype(BF)
                        ring2(d, s, j).start()
            value = landed(7)
            for j in range(2):
                v = value[j]
                for d in range(2):
                    ring2(d, 4, j).wait_recv()
                    v = v + small_r[d, 6 + j].astype(F32)
                total[j] = v
                fin_s[j] = v.astype(BF)
            last = copy(fin_s.at[1 - x], fin_r.at[1], fi_ss.at[1], fi_rs.at[1], x_next)
            last.start()
            last.wait_recv()
            finish(total[x] + fin_r[1].astype(F32))
            last.wait_send()
            for j in range(8):
                ring(j % 2, 1, j).wait_send()
                for d in range(2):
                    ring(d, 2, j).wait_send()
            for s in range(1, 5):
                for j in range(2):
                    for d in range(2):
                        if s > 1 or j == d:
                            ring2(d, s, j).wait_send()

        turned_copy().wait_send()
        for q in range(3):
            dl[q].wait_send()


def shards(token_states, token_ids, master, gain, cand_ids, slab_owner):
    seqs, length, width = token_states.shape[1:]
    tokens = seqs * length
    rows, emb = master.shape[1:]
    vmem = pl.BlockSpec(memory_space=pltpu.VMEM)
    smem = pl.BlockSpec(memory_space=pltpu.SMEM)
    hbm = pl.BlockSpec(memory_space=pl.ANY)
    dma = pltpu.SemaphoreType.DMA
    V = pltpu.VMEM
    out = pl.pallas_call(
        body,
        out_shape=jax.ShapeDtypeStruct((rows, emb), F32),
        in_specs=[hbm, hbm, hbm, vmem, vmem, smem, smem],
        out_specs=vmem,
        scratch_shapes=[
            V((tokens, width), BF),
            V((rows, emb), F32),
            V((1, width), F32),
            V((tokens, width), BF),
            V((NZ, NY, 2, 2, rows, tokens), BF),
            V((NZ, NY, 2, rows, tokens), BF),
            V((NZ, NY, 2, 2, rows, emb), BF),
            V((rows, emb), BF),
            V((tokens, emb), F32),
            V((3, 8, emb // 8), F32),
            V((3, 8, emb // 8), BF),
            V((NZ, NY, 2, 2, 3, 8, emb // 8), BF),
            V((tokens, emb), BF),
            V((tokens, emb), BF),
            V((NZ, 8, rows, emb), F32),
            V((2, rows, emb), F32),
            V((2, 32, rows, emb), BF),
            V((2, 32, rows, emb), BF),
            V((24, rows, emb), BF),
            V((24, rows, emb), BF),
            V((2, 8, rows, emb), BF),
            V((2, 8, rows, emb), BF),
            V((8, rows, emb), BF),
            V((8, rows, emb), BF),
            pltpu.SMEM((24,), jnp.int32),
            dma((3,)),
            dma((4,)), dma((4,)),
            dma((32,)), dma((32,)),
            dma((2, 4, 6)), dma((2, 4, 6)),
            dma((2, 2, 16)), dma((2, 2, 16)),
            dma((64,)), dma((64,)),
            dma, dma,
            dma, dma,
            dma((8,)), dma((8,)),
            dma((16,)), dma((16,)),
            dma((8,)), dma((8,)),
            dma((3,)), dma((3,)),
            dma((2, 24)), dma((2, 24)),
            dma((24,)), dma((24,)),
            dma((2, 8)), dma((2, 8)),
            dma((8,)), dma((8,)),
        ],
        compiler_params=pltpu.CompilerParams(
            collective_id=0, has_side_effects=True, vmem_limit_bytes=62 * 1024 * 1024
        ),
    )(
        token_states.reshape(tokens, width),
        master[0],
        gain.reshape(1, width),
        token_ids.reshape(seqs, 1, length),
        slab_owner.reshape(3, -1),
        cand_ids,
        slab_owner,
    )
    return out[None]


def solution(mesh):
    placed = (
        P("grp", "fsdp", None, None),
        P("grp", "fsdp", None),
        P("grp", "fsdp", None),
        P(),
        P("fsdp", None),
        P(),
    )
    return jax.shard_map(
        shards, mesh=mesh, in_specs=placed, out_specs=P("grp", "fsdp", None), check_vma=False
    )
```

time: 107 us -> 97.7 us (0.913)
  Pallas kernels: 104 us -> 96 us
  local copies, waits for them, and re-layouts: 2.83 us -> 1.57 us
    pallas_call x1, Pallas kernels: 104 us -> 96 us  [shards(): pl.pallas_call(body, out_shape=jax.ShapeDtypeStruct((rows, emb), F32), in...]
    unnamed x2 -> x1, local copies, waits for them, and re-layouts: 2.83 us -> 1.57 us
where the time goes in v2:
time: 97.7 us; the launch traced here: 97.6 us
  Pallas kernels  96 us (98%)
  local copies, waits for them, and re-layouts  1.57 us (2%)
    pallas_call x1, Pallas kernels, shards(): pl.pallas_call(body, out_shape=jax.ShapeDtypeStruct((rows, emb), F32), in...  96 us

profile of v2, /device:TPU:8, one launch (start us, length us, event | category | flops | bytes accessed | tf_op | source)
XLA Modules:
  0.0 97.6 jit_solution(18445492181048496635)
XLA Ops:
  0.0 96.0 %shard_map.64 = f32[32,1024]{1,0:T(8,128)} custom-call(bf16[384,4096]{1,0:T(8,128)(2,1)} %bitcast.6, f32[32,1024]{1,0:T(8,128)} %bitcast.8, f32[1,4096]{1,0:T(1,128)} %bitcast.9, s32[3,1,128]{2,1,0:T(1,128)} %bitcast.11, s32[3,128]{1,0:T(4,128)} %bitcast.10, s32[3,8]{1,0:T(4,128)} %cand_s.1, s32[384]{0:T(512)} %owner_s.1), custom_call_target="tpu_custom_call" | custom-call | tf_op jit(solution)/shard_map/pallas_call | solution.py:641
  96.0 1.6 %copy.8 = f32[1,32,1024]{2,1,0:T(8,128)} copy(f32[1,32,1024]{2,1,0:T(8,128)} %bitcast.7) | data formatting | bytes 262144

commit v3 on v2

--- a/solution.py
+++ b/solution.py
@@ -32,8 +32,8 @@
     states_hbm, master_hbm, gain_hbm, ids_ref, owner_ref, cand_s, owner_s, out_ref,
     states, master, gain, normed, trans, trans_peer, weight, wrecv, act, stage, stored, slab,
     delta, delta_peer, part, total, big_s, big_r, x1_s, x1_r, small_s, small_r, fin_s, fin_r, place_s,
-    ld_sem, ay_s, ay_r, xf_s, xf_r, zr_s, zr_r, yr_s, yr_r, fw_s, fw_r, wt_s, wt_r, tp_s, tp_r,
-    e1_s, e1_r, e2_s, e2_r, e3_s, e3_r, dl_s, dl_r, bg_ss, bg_rs, xx_ss, xx_rs, sm_ss, sm_rs, fi_ss, fi_rs,
+    ld_sem, ag_s, ag_r, fw_s, fw_r, wt_s, wt_r, tp_s, tp_r,
+    e1_s, e1_r, e2_s, e2_r, e3_s, e3_r, dl_s, dl_r, rs_s, rs_r,
 ):
     g = lax.axis_index("grp")
     f = lax.axis_index("fsdp")
@@ -88,8 +88,7 @@
         copy(ref, ref, ssem, rsem, me).wait_send()
 
     def forward(zz, yy, xx, cc):
-        k = ((zz % NZ) * NY + yy % NY) * 2 + xx % 2
-        push(shard(zz, yy, xx, cc), fw_s.at[k], fw_r.at[k], partner)
+        push(shard(zz, yy, xx, cc), fw_s, fw_r, partner)
 
     own = shard(z, y, x, c)
 
@@ -128,97 +127,89 @@
 
         def ring(zz, u, s, d):
             j, i = units[u]
-            push(
-                shard(zz, y + j, x + i, 0), zr_s.at[d, s - 1, u], zr_r.at[d, s - 1, u],
-                dev(z + STEP[d], y, x, 0),
-            )
-
-        def cross(zz, j):
-            k = (zz % NZ) * NY + j
-            push(shard(zz, y + j, x, 0), xf_s.at[k], xf_r.at[k], x_next)
-
-        def crossed(zz, j):
-            k = (zz % NZ) * NY + j
-            got(shard(zz, y + j, x + 1, 0), xf_s.at[k], xf_r.at[k])
-            forward(zz, y + j, x + 1, 0)
+            push(shard(zz, y + j, x + i, 0), ag_s, ag_r.at[place(d, s, u)], dev(z + STEP[d], y, x, 0))
+
+        def place(d, s, u):
+            n = len(units)
+            return (s - 1) * 2 * n + d * n + u if s < 4 else 6 * n + u
+
+        base = 7 * len(units)
+
+        def spot(k, j):
+            return base + (0 if j == 0 else 1 + k * len(AG_XL) + AG_XL.index(j))
+
+        def cross(k, j):
+            push(shard(z + OFFS[k], y + j, x, 0), ag_s, ag_r.at[spot(k, j)], x_next)
+
+        def crossed(k, j):
+            got(shard(z + OFFS[k], y + j, x + 1, 0), ag_s, ag_r.at[spot(k, j)])
+            forward(z + OFFS[k], y + j, x + 1, 0)
+
+        side = base + 1 + NZ * len(AG_XL)
 
         for d in range(2):
             ring(z, 0, 1, d)
-        cross(z, 0)
+        cross(0, 0)
         for j in (1, 3, 2):
-            push(own, ay_s.at[j], ay_r.at[j], dev(z, y + j, x, 0))
+            push(own, ag_s, ag_r.at[side + j - 1], dev(z, y + j, x, 0))
         forward(z, y, x, 0)
         norm()
-        crossed(z, 0)
+        crossed(0, 0)
         for d in range(2):
             ring(z, units.index((0, 1)), 1, d)
         for j in (1, 3, 2):
-            got(shard(z, y + j, x, 0), ay_s.at[(-j) % NY], ay_r.at[(-j) % NY])
+            got(shard(z, y + j, x, 0), ag_s, ag_r.at[side + (-j) % NY - 1])
             for d in range(2):
                 ring(z, units.index((j, 0)), 1, d)
-            cross(z, j)
+            cross(0, j)
             forward(z, y + j, x, 0)
-        for j in (1, 3, 2):
-            if j not in AG_XL:
-                crossed(z, j)
-                for d in range(2):
-                    ring(z, units.index((j, 1)), 1, d)
         transpose(0, 2)
 
-        def serve(zz, first):
+        def serve(k):
             for j in AG_XL:
-                crossed(zz, j)
+                crossed(k, j)
 
         for s in range(2, 5):
             for u, (j, i) in enumerate(units):
                 for d in range(2):
                     zz = z - STEP[d] * (s - 1)
-                    got(shard(zz, y + j, x + i, 0), zr_s.at[d, s - 2, u], zr_r.at[d, s - 2, u])
+                    got(shard(zz, y + j, x + i, 0), ag_s, ag_r.at[place(d, s - 1, u)])
                     if s < 4 or u % 2 == d:
                         ring(zz, u, s, d)
                     if j in AG_XL:
-                        cross(zz, j)
+                        cross(2 * s - 3 + d, j)
                     forward(zz, y + j, x + i, 0)
-            if s == 2:
-                serve(z, True)
-            else:
-                for d in range(2):
-                    serve(z - STEP[d] * (s - 2), False)
+            for k in (0,) if s == 2 else (2 * s - 5, 2 * s - 4):
+                serve(k)
             transpose(2 * s - 2, 2 * s)
         for u, (j, i) in enumerate(units):
-            d = u % 2
-            got(shard(z + 4, y + j, x + i, 0), zr_s.at[d, 3, u], zr_r.at[d, 3, u])
+            got(shard(z + 4, y + j, x + i, 0), ag_s, ag_r.at[place(u % 2, 4, u)])
             if j in AG_XL:
-                cross(z + 4, j)
+                cross(7, j)
             forward(z + 4, y + j, x + i, 0)
         weight_start()
-        for zz in (z - 3, z + 3, z + 4):
-            serve(zz, False)
-        for j in (1, 3, 2):
-            sent(own, ay_s.at[j], ay_r.at[j])
-        for u in range(len(units)):
-            for s in range(1, 5):
-                for d in range(2):
-                    if s < 4 or u % 2 == d:
-                        sent(own, zr_s.at[d, s - 1, u], zr_r.at[d, s - 1, u])
-        for off in range(NZ):
-            for j in range(NY):
-                if j in AG_XL or off == 0:
-                    k = ((z + off) % NZ) * NY + j
-                    sent(own, xf_s.at[k], xf_r.at[k])
+        for k in (5, 6, 7):
+            serve(k)
+        sent(big_s.at[pl.ds(0, 7 * len(units) + 1 + NZ * len(AG_XL) + 3)], ag_s, ag_r.at[0])
 
     @pl.when(c == 1)
     def _():
         def ring(zz, i, s, d):
-            push(
-                shard(zz, y, x + i, 1), zr_s.at[d, s - 1, i], zr_r.at[d, s - 1, i],
-                dev(z + STEP[d], y, x, 1),
-            )
+            push(shard(zz, y, x + i, 1), ag_s, ag_r.at[place(d, s, i)], dev(z + STEP[d], y, x, 1))
+
+        def place(d, s, i):
+            return (s - 1) * 4 + d * 2 + i if s < 4 else 12 + i
+
+        def near(d, k, i):
+            return 14 + d * 16 + 2 * k + i
+
+        def far(d, k):
+            return 46 + d * 8 + k
 
         def spread(k, i):
             ref = shard(z + OFFS[k], y, x + i, 1)
             for d in range(2):
-                push(ref, yr_s.at[d, 0, 2 * k + i], yr_r.at[d, 0, 2 * k + i], dev(z, y + STEP[d], x, 1))
+                push(ref, ag_s, ag_r.at[near(d, k, i)], dev(z, y + STEP[d], x, 1))
             forward(z + OFFS[k], y, x + i, 1)
 
         def serve(k):
@@ -226,17 +217,17 @@
                 for d in range(2):
                     yy = y - STEP[d]
                     ref = shard(z + OFFS[k], yy, x + i, 1)
-                    got(ref, yr_s.at[d, 0, 2 * k + i], yr_r.at[d, 0, 2 * k + i])
+                    got(ref, ag_s, ag_r.at[near(d, k, i)])
                     if i == d:
-                        push(ref, yr_s.at[d, 1, k], yr_r.at[d, 1, k], dev(z, y + STEP[d], x, 1))
+                        push(ref, ag_s, ag_r.at[far(d, k)], dev(z, y + STEP[d], x, 1))
                     forward(z + OFFS[k], yy, x + i, 1)
 
-        push(own, ay_s.at[0], ay_r.at[0], x_next)
+        push(own, ag_s, ag_r.at[62], x_next)
         for d in range(2):
             ring(z, 0, 1, d)
         spread(0, 0)
         norm()
-        got(shard(z, y, x + 1, 1), ay_s.at[0], ay_r.at[0])
+        got(shard(z, y, x + 1, 1), ag_s, ag_r.at[62])
         for d in range(2):
             ring(z, 1, 1, d)
         spread(0, 1)
@@ -245,7 +236,7 @@
             for d in range(2):
                 zz = z - STEP[d] * (s - 1)
                 for i in range(2):
-                    got(shard(zz, y, x + i, 1), zr_s.at[d, s - 2, i], zr_r.at[d, s - 2, i])
+                    got(shard(zz, y, x + i, 1), ag_s, ag_r.at[place(d, s - 1, i)])
                     if s < 4 or i == d:
                         ring(zz, i, s, d)
                     spread(2 * s - 3 + d, i)
@@ -253,7 +244,7 @@
                 serve(k)
             transpose(2 * s - 3, 2 * s - 1)
         for i in range(2):
-            got(shard(z + 4, y, x + i, 1), zr_s.at[i, 3, i], zr_r.at[i, 3, i])
+            got(shard(z + 4, y, x + i, 1), ag_s, ag_r.at[place(i, 4, i)])
             spread(7, i)
         weight_start()
         transpose(7, 8)
@@ -261,19 +252,9 @@
             serve(k)
         for k in range(NZ):
             for d in range(2):
-                got(shard(z + OFFS[k], y + 2, x + d, 1), yr_s.at[d, 1, k], yr_r.at[d, 1, k])
+                got(shard(z + OFFS[k], y + 2, x + d, 1), ag_s, ag_r.at[far(d, k)])
                 forward(z + OFFS[k], y + 2, x + d, 1)
-        sent(own, ay_s.at[0], ay_r.at[0])
-        for s in range(1, 5):
-            for i in range(2):
-                for d in range(2):
-                    if s < 4 or i == d:
-                        sent(own, zr_s.at[d, s - 1, i], zr_r.at[d, s - 1, i])
-        for k in range(NZ):
-            for d in range(2):
-                for i in range(2):
-                    sent(own, yr_s.at[d, 0, 2 * k + i], yr_r.at[d, 0, 2 * k + i])
-                sent(own, yr_s.at[d, 1, k], yr_r.at[d, 1, k])
+        sent(big_s.at[pl.ds(0, 63)], ag_s, ag_r.at[0])
 
     def turned_copy():
         return copy(trans.at[:, :, :, 1 - c], trans_peer, tp_s, tp_r, partner)
@@ -292,11 +273,7 @@
                 same = (owner_ref[...] == owner) & (position < row)
                 place_s[q * 8 + j] = owner * 3 + jnp.sum(same.astype(jnp.int32))
 
-    def fw_got(k, carry):
-        got(weight.at[k // 8, (k // 2) % NY, k % 2, 1 - c], fw_s.at[k], fw_r.at[k])
-        return carry
-
-    lax.fori_loop(0, 64, fw_got, 0)
+    got(weight.at[:, :, :, 1 - c], fw_s, fw_r)
 
     def hidden_step(n, carry):
         columns = pl.ds(pl.multiple_of(n * 256, 256), 256)
@@ -307,11 +284,7 @@
 
     lax.fori_loop(0, emb // 256, hidden_step, 0)
 
-    def fw_sent(k, carry):
-        sent(weight.at[k // 8, (k // 2) % NY, k % 2, c], fw_s.at[k], fw_r.at[k])
-        return carry
-
-    lax.fori_loop(0, 64, fw_sent, 0)
+    sent(weight.at[:, :, :, c], fw_s, fw_r)
 
     lanes = emb // 8
     length = tokens // 3
@@ -338,52 +311,40 @@
         scales.append(scale)
         units.append(pool * scale)
 
-    def e1(zz):
-        return copy(stored, slab.at[z, y, x, c], e1_s.at[zz % NZ], e1_r.at[z], dev(zz, y, x, c, 0))
-
     @pl.when(g == 1)
     def _():
         for q in range(3):
             stored[q] = units[q].astype(BF)
         weight_copy().wait_recv()
-        for off in (4, 3, -3, 2, -2, 1, -1, 0):
-            e1(z + off).start()
+        for b in (1, 0):
+            for off in (NEAR, FAR)[b]:
+                to = dev(z + off, y, x, c, 0)
+                copy(stored, slab.at[z, y, x, c], e1_s, e1_r.at[b], to).start()
         out_ref[...] = wrecv[...].astype(F32)
-        for zz in range(NZ):
-            e1(zz).wait_send()
+        sent(slab.at[:, 0, 0, 0], e1_s, e1_r.at[0])
 
     @pl.when(trainer)
     def _():
-        rels = [(dy, dx) for dy in range(NY) for dx in range(2)]
         sends = [(2, 0), (2, 1), (1, 0), (3, 0), (1, 1), (3, 1), (0, 1)]
 
         def e2(b, dy, dx):
-            k = b * 8 + dy * 2 + dx
             to = dev(z, y + dy, (x + dx) % 2, c)
             for off in (NEAR, FAR)[b]:
-                ref = slab.at[(z + off) % NZ, y, x, c]
-                push(ref, e2_s.at[k], e2_r.at[k], to)
-
-        def e3(yy, xx, k, cc):
-            ref = slab.at[:, yy % NY, xx, cc]
-            return copy(ref, ref, e3_s.at[k], e3_r.at[k], partner)
+                push(slab.at[(z + off) % NZ, y, x, c], e2_s, e2_r.at[dy * 2 + dx], to)
+
+        def e3(yy, xx):
+            push(slab.at[:, yy % NY, xx, c], e3_s, e3_r, partner)
 
         for b in range(2):
-            for off in (NEAR, FAR)[b]:
-                zz = (z + off) % NZ
-                got(slab.at[zz, y, x, c], e1_s.at[zz], e1_r.at[zz])
+            got(slab.at[0 : len((NEAR, FAR)[b]), y, x, c], e1_s, e1_r.at[b])
             for dy, dx in sends:
                 e2(b, dy, dx)
-        e3(y, x, 0, c).start()
+        e3(y, x)
         for dy, dx in ((0, 1), (1, 0), (3, 0), (1, 1), (3, 1), (2, 0), (2, 1)):
-            k = dy * 2 + dx
             yy, xx = (y - dy) % NY, (x + dx) % 2
-            got(slab.at[0:5, yy, xx, c], e2_s.at[k], e2_r.at[k])
-            got(slab.at[0:3, yy, xx, c], e2_s.at[8 + k], e2_r.at[8 + k])
-            e3(yy, xx, k, c).start()
-        for dy, dx in rels:
-            k = dy * 2 + dx
-            e3(y - dy, (x + dx) % 2, k, 1 - c).wait_recv()
+            got(slab.at[:, yy, xx, c], e2_s, e2_r.at[dy * 2 + dx])
+            e3(yy, xx)
+        got(slab.at[:, :, :, 1 - c], e3_s, e3_r)
         for q in range(3):
             rows, exps = [], []
             for j in range(8):
@@ -411,20 +372,15 @@
                 a = act[span, cols]
                 base = jnp.where(masks[q], 1.0 / counts[q], 0.0) * stage[q, k : k + 1, :]
                 delta[span, cols] = (base * (1.0 - a * a)).astype(BF)
-            dl.append(copy(delta.at[span], delta_peer.at[span], dl_s.at[q], dl_r.at[q], partner))
+            dl.append(copy(delta.at[span], delta_peer.at[span], dl_s, dl_r, partner))
             if q > 0:
                 dl[q - 1].start()
         dl[2].start()
-        for dy, dx in rels:
-            k = dy * 2 + dx
-            if k:
-                sent(slab.at[0:5, y, x, c], e2_s.at[k], e2_r.at[k])
-                sent(slab.at[0:3, y, x, c], e2_s.at[8 + k], e2_r.at[8 + k])
-            e3(y - dy, (x + dx) % 2, k, c).wait_send()
+        sent(slab.at[0:7, :, :, 0], e2_s, e2_r.at[0])
+        sent(slab.at[:, :, :, c], e3_s, e3_r)
         weight_copy().wait_send()
         turned_copy().wait_recv()
-        for q in range(3):
-            dl[q].wait_recv()
+        got(delta, dl_s, dl_r)
 
         def unit(u, lhs, lhs_peer):
             value = jnp.dot(lhs.reshape(256, tokens), delta[...], preferred_element_type=F32)
@@ -445,7 +401,7 @@
 
             def x_first(b, n):
                 k = b * 3 + n
-                return copy(x1_s.at[k], x1_r.at[k], xx_ss.at[k], xx_rs.at[k], x_next)
+                return copy(x1_s.at[k], x1_r.at[k], rs_s, rs_r.at[k], x_next)
 
             def compute(b, carry):
                 odd = b % 2
@@ -463,11 +419,11 @@
                 return carry
 
             def ring(d, s, u):
-                k = (s - 1) * count + u
-                return copy(
-                    big_s.at[d, k], big_r.at[d, k], bg_ss.at[d, k], bg_rs.at[d, k],
-                    dev(z + STEP[d], y, x, 0),
-                )
+                k = spot(d, s, u)
+                return copy(big_s.at[k], big_r.at[k], rs_s, rs_r.at[24 + k], dev(z + STEP[d], y, x, 0))
+
+            def spot(d, s, u):
+                return u if s == 1 else count + (s - 2) * 2 * count + d * count + u
 
             def local(b, u):
                 j, i = pairs[u]
@@ -480,7 +436,7 @@
 
             def first(u):
                 d = u % 2
-                big_s[d, u] = local(0, u).astype(BF)
+                big_s[spot(d, 1, u)] = local(0, u).astype(BF)
                 ring(d, 1, u).start()
 
             plain = [u for u, (j, i) in enumerate(pairs) if j not in RS_XL]
@@ -495,26 +451,24 @@
             for s in range(2, 5):
                 for u in range(count):
                     for d in range(2):
-                        k = (s - 1) * count + u
                         value = local(2 * s - 3 + d, u)
                         if s > 2 or u % 2 == d:
                             ring(d, s - 1, u).wait_recv()
-                            value = value + big_r[d, k - count].astype(F32)
-                        big_s[d, k] = value.astype(BF)
+                            value = value + big_r[spot(d, s - 1, u)].astype(F32)
+                        big_s[spot(d, s, u)] = value.astype(BF)
                         ring(d, s, u).start()
 
             def last(j, i):
                 k = j * 2 + i
-                return copy(
-                    fin_s.at[k], fin_r.at[k], fi_ss.at[k], fi_rs.at[k], dev(z, y + j, (x + i) % 2, 0)
-                )
+                n = 24 + 7 * count + pairs.index((j, i)) - 1
+                return copy(fin_s.at[k], fin_r.at[k], rs_s, rs_r.at[n], dev(z, y + j, (x + i) % 2, 0))
 
             for u in list(range(1, count)) + [0]:
                 j, i = pairs[u]
                 value = local(7, u)
                 for d in range(2):
                     ring(d, 4, u).wait_recv()
-                    value = value + big_r[d, 3 * count + u].astype(F32)
+                    value = value + big_r[spot(d, 4, u)].astype(F32)
                 if u:
                     fin_s[j * 2 + i] = value.astype(BF)
                     last(j, i).start()
@@ -525,16 +479,7 @@
                 last(j, i).wait_recv()
                 value = value + fin_r[j * 2 + i].astype(F32)
             finish(value)
-            for j, i in pairs[1:]:
-                last(j, i).wait_send()
-            for b in range(NZ):
-                for n in range(len(RS_XL)):
-                    x_first(b, n).wait_send()
-            for s in range(1, 5):
-                for u in range(count):
-                    for d in range(2):
-                        if s > 1 or u % 2 == d:
-                            ring(d, s, u).wait_send()
+            sent(big_s.at[pl.ds(0, 24 + 8 * count - 1)], rs_s, rs_r.at[0])
 
         @pl.when(c == 1)
         def _():
@@ -550,16 +495,21 @@
                 return part[(yy % NY) * 2 + zz // 4, pl.ds((zz % 4) * 2, 2)]
 
             def ring(d, s, j):
-                k = (s - 1) * 8 + j
+                k = spot(d, s, j)
                 span = pl.ds(2 * k, 2)
                 return copy(
-                    big_s.at[d, span], big_r.at[d, span], bg_ss.at[d, k], bg_rs.at[d, k],
-                    dev(z, y + STEP[d], x, 1),
+                    big_s.at[span], big_r.at[span], rs_s, rs_r.at[k], dev(z, y + STEP[d], x, 1)
                 )
+
+            def spot(d, s, j):
+                return j if s == 1 else 8 + d * 8 + j
+
+            def place(d, s, j):
+                return pl.ds(2 * spot(d, s, j), 2)
 
             lax.fori_loop(0, 2, compute, 0)
             for j in range(8):
-                big_s[j % 2, 2 * j : 2 * j + 2] = local(y + 2, j).astype(BF)
+                big_s[place(j % 2, 1, j)] = local(y + 2, j).astype(BF)
                 ring(j % 2, 1, j).start()
             lax.fori_loop(2, NZ, compute, 0)
             for j in range(8):
@@ -567,21 +517,21 @@
                     value = local(y + STEP[d], j)
                     if j % 2 == d:
                         ring(d, 1, j).wait_recv()
-                        value = value + big_r[d, 2 * j : 2 * j + 2].astype(F32)
-                    big_s[d, 16 + 2 * j : 18 + 2 * j] = value.astype(BF)
+                        value = value + big_r[place(d, 1, j)].astype(F32)
+                    big_s[place(d, 2, j)] = value.astype(BF)
                     ring(d, 2, j).start()
 
             def landed(j):
                 value = local(y, j)
                 for d in range(2):
                     ring(d, 2, j).wait_recv()
-                    value = value + big_r[d, 16 + 2 * j : 18 + 2 * j].astype(F32)
+                    value = value + big_r[place(d, 2, j)].astype(F32)
                 return value
 
             def ring2(d, s, j):
                 k = (s - 1) * 2 + j
                 return copy(
-                    small_s.at[d, k], small_r.at[d, k], sm_ss.at[d, k], sm_rs.at[d, k],
+                    small_s.at[d, k], small_r.at[d, k], rs_s, rs_r.at[24 + d * 8 + k],
                     dev(z + STEP[d], y, x, 1),
                 )
 
@@ -609,24 +559,14 @@
                     v = v + small_r[d, 6 + j].astype(F32)
                 total[j] = v
                 fin_s[j] = v.astype(BF)
-            last = copy(fin_s.at[1 - x], fin_r.at[1], fi_ss.at[1], fi_rs.at[1], x_next)
+            last = copy(fin_s.at[1 - x], fin_r.at[1], rs_s, rs_r.at[40], x_next)
             last.start()
             last.wait_recv()
             finish(total[x] + fin_r[1].astype(F32))
-            last.wait_send()
-            for j in range(8):
-                ring(j % 2, 1, j).wait_send()
-                for d in range(2):
-                    ring(d, 2, j).wait_send()
-            for s in range(1, 5):
-                for j in range(2):
-                    for d in range(2):
-                        if s > 1 or j == d:
-                            ring2(d, s, j).wait_send()
+            sent(big_s.at[pl.ds(0, 63)], rs_s, rs_r.at[0])
 
         turned_copy().wait_send()
-        for q in range(3):
-            dl[q].wait_send()
+        sent(delta, dl_s, dl_r)
 
 
 def shards(token_states, token_ids, master, gain, cand_ids, slab_owner):
@@ -660,8 +600,8 @@
             V((tokens, emb), BF),
             V((NZ, 8, rows, emb), F32),
             V((2, rows, emb), F32),
-            V((2, 32, rows, emb), BF),
-            V((2, 32, rows, emb), BF),
+            V((64, rows, emb), BF),
+            V((64, rows, emb), BF),
             V((24, rows, emb), BF),
             V((24, rows, emb), BF),
             V((2, 8, rows, emb), BF),
@@ -670,21 +610,15 @@
             V((8, rows, emb), BF),
             pltpu.SMEM((24,), jnp.int32),
             dma((3,)),
-            dma((4,)), dma((4,)),
-            dma((32,)), dma((32,)),
-            dma((2, 4, 6)), dma((2, 4, 6)),
-            dma((2, 2, 16)), dma((2, 2, 16)),
-            dma((64,)), dma((64,)),
+            dma, dma((64,)),
             dma, dma,
             dma, dma,
-            dma((8,)), dma((8,)),
-            dma((16,)), dma((16,)),
-            dma((8,)), dma((8,)),
-            dma((3,)), dma((3,)),
-            dma((2, 24)), dma((2, 24)),
-            dma((24,)), dma((24,)),
-            dma((2, 8)), dma((2, 8)),
-            dma((8,)), dma((8,)),
+            dma, dma,
+            dma, dma((2,)),
+            dma, dma((8,)),
+            dma, dma,
+            dma, dma,
+            dma, dma((64,)),
         ],
         compiler_params=pltpu.CompilerParams(
             collective_id=0, has_side_effects=True, vmem_limit_bytes=62 * 1024 * 1024

time: 97.7 us -> 91.9 us (0.941)
  Pallas kernels: 96 us -> 90.2 us
    pallas_call x1, Pallas kernels: 96 us -> 90.2 us  [shards(): pl.pallas_call(body, out_shape=jax.ShapeDtypeStruct((rows, emb), F32), in...]
where the time goes in v3:
time: 91.9 us; the launch traced here: 91.8 us
  Pallas kernels  90.2 us (98%)
  local copies, waits for them, and re-layouts  1.57 us (2%)
    pallas_call x1, Pallas kernels, shards(): pl.pallas_call(body, out_shape=jax.ShapeDtypeStruct((rows, emb), F32), in...  90.2 us

profile of v3, /device:TPU:8, one launch (start us, length us, event | category | flops | bytes accessed | tf_op | source)
XLA Modules:
  0.0 91.8 jit_solution(6103105122530832898)
XLA Ops:
  0.0 90.2 %shard_map.64 = f32[32,1024]{1,0:T(8,128)} custom-call(bf16[384,4096]{1,0:T(8,128)(2,1)} %bitcast.6, f32[32,1024]{1,0:T(8,128)} %bitcast.8, f32[1,4096]{1,0:T(1,128)} %bitcast.9, s32[3,1,128]{2,1,0:T(1,128)} %bitcast.11, s32[3,128]{1,0:T(4,128)} %bitcast.10, s32[3,8]{1,0:T(4,128)} %cand_s.1, s32[384]{0:T(512)} %owner_s.1), custom_call_target="tpu_custom_call" | custom-call | tf_op jit(solution)/shard_map/pallas_call | solution.py:581
  90.2 1.6 %copy.8 = f32[1,32,1024]{2,1,0:T(8,128)} copy(f32[1,32,1024]{2,1,0:T(8,128)} %bitcast.7) | data formatting | bytes 262144

commit v4 on v3

--- a/solution.py
+++ b/solution.py
@@ -31,9 +31,9 @@
 def body(
     states_hbm, master_hbm, gain_hbm, ids_ref, owner_ref, cand_s, owner_s, out_ref,
     states, master, gain, normed, trans, trans_peer, weight, wrecv, act, stage, stored, slab,
-    delta, delta_peer, part, total, big_s, big_r, x1_s, x1_r, small_s, small_r, fin_s, fin_r, place_s,
+    delta, delta_peer, act_peer, ids_peer, stage_peer, part, total, big_s, big_r, x1_s, x1_r, small_s, small_r, fin_s, fin_r, place_s,
     ld_sem, ag_s, ag_r, fw_s, fw_r, wt_s, wt_r, tp_s, tp_r,
-    e1_s, e1_r, e2_s, e2_r, e3_s, e3_r, dl_s, dl_r, rs_s, rs_r,
+    e1_s, e1_r, e2_s, e2_r, e3_s, e3_r, dl_s, dl_r, ac_s, ac_r, rs_s, rs_r,
 ):
     g = lax.axis_index("grp")
     f = lax.axis_index("fsdp")
@@ -111,7 +111,9 @@
         return carry
 
     def transpose(lo, hi):
-        lax.fori_loop(lo, hi, transpose_step, 0)
+        @pl.when(trainer)
+        def _():
+            lax.fori_loop(lo, hi, transpose_step, 0)
 
     def weight_copy():
         return copy(own, wrecv, wt_s, wt_r, (1 - g, f))
@@ -176,6 +178,9 @@
                     got(shard(zz, y + j, x + i, 0), ag_s, ag_r.at[place(d, s - 1, u)])
                     if s < 4 or u % 2 == d:
                         ring(zz, u, s, d)
+                    if s == 4 and u % 2 == d and j in AG_XL:
+                        to = dev(z + STEP[d], y, 1 - x, 0)
+                        push(shard(zz, y + j, x, 0), ag_s, ag_r.at[spot(7, j)], to)
                     if j in AG_XL:
                         cross(2 * s - 3 + d, j)
                     forward(zz, y + j, x + i, 0)
@@ -184,8 +189,6 @@
             transpose(2 * s - 2, 2 * s)
         for u, (j, i) in enumerate(units):
             got(shard(z + 4, y + j, x + i, 0), ag_s, ag_r.at[place(u % 2, 4, u)])
-            if j in AG_XL:
-                cross(7, j)
             forward(z + 4, y + j, x + i, 0)
         weight_start()
         for k in (5, 6, 7):
@@ -210,6 +213,8 @@
             ref = shard(z + OFFS[k], y, x + i, 1)
             for d in range(2):
                 push(ref, ag_s, ag_r.at[near(d, k, i)], dev(z, y + STEP[d], x, 1))
+            if k == 7:
+                push(ref, ag_s, ag_r.at[far(i, k)], dev(z, y + 2, x, 1))
             forward(z + OFFS[k], y, x + i, 1)
 
         def serve(k):
@@ -218,7 +223,7 @@
                     yy = y - STEP[d]
                     ref = shard(z + OFFS[k], yy, x + i, 1)
                     got(ref, ag_s, ag_r.at[near(d, k, i)])
-                    if i == d:
+                    if i == d and k < 7:
                         push(ref, ag_s, ag_r.at[far(d, k)], dev(z, y + STEP[d], x, 1))
                     forward(z + OFFS[k], yy, x + i, 1)
 
@@ -259,9 +264,16 @@
     def turned_copy():
         return copy(trans.at[:, :, :, 1 - c], trans_peer, tp_s, tp_r, partner)
 
+    def act_copies():
+        return (
+            copy(ids_ref, ids_peer, ac_s.at[0], ac_r.at[0], partner),
+            copy(act, act_peer, ac_s.at[1], ac_r.at[1], partner),
+        )
+
     @pl.when(trainer)
     def _():
         turned_copy().start()
+        act_copies()[0].start()
         position = (
             lax.broadcasted_iota(jnp.int32, owner_ref.shape, 0) * owner_ref.shape[1]
             + lax.broadcasted_iota(jnp.int32, owner_ref.shape, 1)
@@ -285,6 +297,10 @@
     lax.fori_loop(0, emb // 256, hidden_step, 0)
 
     sent(weight.at[:, :, :, c], fw_s, fw_r)
+
+    @pl.when(trainer)
+    def _():
+        act_copies()[1].start()
 
     lanes = emb // 8
     length = tokens // 3
@@ -364,23 +380,30 @@
             inner = full_sum(pooled[q] * grad)
             scale = scales[q]
             stage[q] = scale * grad - pooled[q] * (scale * scale * scale) * inner * (1.0 / emb)
-        dl = []
-        for q in range(3):
+        def fill(q, count, mask, act_ref, stage_ref, delta_ref):
             span = slice(q * length, (q + 1) * length)
             for k in range(8):
                 cols = slice(k * lanes, (k + 1) * lanes)
-                a = act[span, cols]
-                base = jnp.where(masks[q], 1.0 / counts[q], 0.0) * stage[q, k : k + 1, :]
-                delta[span, cols] = (base * (1.0 - a * a)).astype(BF)
-            dl.append(copy(delta.at[span], delta_peer.at[span], dl_s, dl_r, partner))
-            if q > 0:
-                dl[q - 1].start()
-        dl[2].start()
+                a = act_ref[span, cols]
+                base = jnp.where(mask, 1.0 / count, 0.0) * stage_ref[q, k : k + 1, :]
+                delta_ref[span, cols] = (base * (1.0 - a * a)).astype(BF)
+
+        grads = copy(stage, stage_peer, dl_s, dl_r, partner)
+        for q in range(3):
+            fill(q, counts[q], masks[q], act, stage, delta)
+            if q == 0:
+                grads.start()
+        for pending in act_copies():
+            pending.wait()
+        grads.wait()
+        for q in range(3):
+            valid = (ids_peer[q] != 0).astype(jnp.int32)
+            count = jnp.sum(valid, axis=1, keepdims=True)
+            fill(q, count.astype(F32), places < count, act_peer, stage_peer, delta_peer)
         sent(slab.at[0:7, :, :, 0], e2_s, e2_r.at[0])
         sent(slab.at[:, :, :, c], e3_s, e3_r)
         weight_copy().wait_send()
         turned_copy().wait_recv()
-        got(delta, dl_s, dl_r)
 
         def unit(u, lhs, lhs_peer):
             value = jnp.dot(lhs.reshape(256, tokens), delta[...], preferred_element_type=F32)
@@ -393,7 +416,7 @@
 
         @pl.when(c == 0)
         def _():
-            pairs = units_of(RS_XL)
+            pairs = [units_of(RS_XL)[q] for q in (1, 2, 3, 4, 0)]
             count = len(pairs)
 
             def slot(j, i):
@@ -402,6 +425,11 @@
             def x_first(b, n):
                 k = b * 3 + n
                 return copy(x1_s.at[k], x1_r.at[k], rs_s, rs_r.at[k], x_next)
+
+            def diagonal(n):
+                d = pairs.index((RS_XL[n], 0)) % 2
+                to = dev(z + STEP[d], y, 1 - x, 0)
+                return copy(x1_s.at[n], x1_r.at[n], rs_s, rs_r.at[n], to)
 
             def compute(b, carry):
                 odd = b % 2
@@ -428,7 +456,7 @@
             def local(b, u):
                 j, i = pairs[u]
                 value = part[(z + RS_OFFS[b]) % NZ, slot(j, i)]
-                if j in RS_XL:
+                if j in RS_XL and b:
                     n = RS_XL.index(j)
                     x_first(b, n).wait_recv()
                     value = value + x1_r[b * 3 + n].astype(F32)
@@ -439,15 +467,12 @@
                 big_s[spot(d, 1, u)] = local(0, u).astype(BF)
                 ring(d, 1, u).start()
 
-            plain = [u for u, (j, i) in enumerate(pairs) if j not in RS_XL]
-            compute_send(0, 0)
-            for u in plain:
+            compute(0, 0)
+            for u in range(count):
                 first(u)
-            lax.fori_loop(1, 4, compute_send, 0)
-            for u in range(count):
-                if u not in plain:
-                    first(u)
-            lax.fori_loop(4, NZ, compute_send, 0)
+            for n in range(len(RS_XL)):
+                diagonal(n).start()
+            lax.fori_loop(1, NZ, compute_send, 0)
             for s in range(2, 5):
                 for u in range(count):
                     for d in range(2):
@@ -455,27 +480,31 @@
                         if s > 2 or u % 2 == d:
                             ring(d, s - 1, u).wait_recv()
                             value = value + big_r[spot(d, s - 1, u)].astype(F32)
+                        if s == 2 and u % 2 == d and pairs[u][0] in RS_XL:
+                            n = RS_XL.index(pairs[u][0])
+                            diagonal(n).wait_recv()
+                            value = value + x1_r[n].astype(F32)
                         big_s[spot(d, s, u)] = value.astype(BF)
                         ring(d, s, u).start()
 
             def last(j, i):
                 k = j * 2 + i
-                n = 24 + 7 * count + pairs.index((j, i)) - 1
+                n = 24 + 7 * count + pairs.index((j, i))
                 return copy(fin_s.at[k], fin_r.at[k], rs_s, rs_r.at[n], dev(z, y + j, (x + i) % 2, 0))
 
-            for u in list(range(1, count)) + [0]:
+            for u in range(count):
                 j, i = pairs[u]
                 value = local(7, u)
                 for d in range(2):
                     ring(d, 4, u).wait_recv()
                     value = value + big_r[spot(d, 4, u)].astype(F32)
-                if u:
+                if u < count - 1:
                     fin_s[j * 2 + i] = value.astype(BF)
                     last(j, i).start()
                 else:
                     total[0] = value
             value = total[0]
-            for j, i in pairs[1:]:
+            for j, i in pairs[-2::-1]:
                 last(j, i).wait_recv()
                 value = value + fin_r[j * 2 + i].astype(F32)
             finish(value)
@@ -497,9 +526,8 @@
             def ring(d, s, j):
                 k = spot(d, s, j)
                 span = pl.ds(2 * k, 2)
-                return copy(
-                    big_s.at[span], big_r.at[span], rs_s, rs_r.at[k], dev(z, y + STEP[d], x, 1)
-                )
+                to = dev(z, y + (2 if s == 1 and j == 0 else STEP[d]), x, 1)
+                return copy(big_s.at[span], big_r.at[span], rs_s, rs_r.at[k], to)
 
             def spot(d, s, j):
                 return j if s == 1 else 8 + d * 8 + j
@@ -515,58 +543,62 @@
             for j in range(8):
                 for d in range(2):
                     value = local(y + STEP[d], j)
-                    if j % 2 == d:
+                    if j and j % 2 == d:
                         ring(d, 1, j).wait_recv()
                         value = value + big_r[place(d, 1, j)].astype(F32)
                     big_s[place(d, 2, j)] = value.astype(BF)
                     ring(d, 2, j).start()
 
             def landed(j):
-                value = local(y, j)
+                if j == 0:
+                    ring(0, 1, 0).wait_recv()
                 for d in range(2):
                     ring(d, 2, j).wait_recv()
-                    value = value + big_r[place(d, 2, j)].astype(F32)
+
+            def piece(j, i):
+                zz = (z + RS_OFFS[j]) % NZ
+                side = (x + i) % 2
+                value = part[y * 2 + zz // 4, (zz % 4) * 2 + side]
+                if j == 0:
+                    value = value + big_r[side].astype(F32)
+                for d in range(2):
+                    value = value + big_r[2 * spot(d, 2, j) + side].astype(F32)
                 return value
 
-            def ring2(d, s, j):
-                k = (s - 1) * 2 + j
-                return copy(
-                    small_s.at[d, k], small_r.at[d, k], rs_s, rs_r.at[24 + d * 8 + k],
-                    dev(z + STEP[d], y, x, 1),
-                )
-
-            value = landed(0)
-            for j in range(2):
-                small_s[j, j] = value[j].astype(BF)
-            for j in range(2):
-                ring2(j, 1, j).start()
+            def ring2(d, s, i):
+                k = (s - 1) * 2 + i
+                to = dev(z + STEP[d], y, (x + (i if s == 4 else 0)) % 2, 1)
+                return copy(small_s.at[d, k], small_r.at[d, k], rs_s, rs_r.at[24 + d * 8 + k], to)
+
+            landed(0)
+            for i in range(2):
+                small_s[i, i] = piece(0, i).astype(BF)
+                ring2(i, 1, i).start()
             for s in range(2, 5):
                 for d in range(2):
-                    value = landed(2 * s - 3 + d)
-                    for j in range(2):
-                        k = (s - 1) * 2 + j
-                        v = value[j]
-                        if s > 2 or j == d:
-                            ring2(d, s - 1, j).wait_recv()
-                            v = v + small_r[d, k - 2].astype(F32)
-                        small_s[d, k] = v.astype(BF)
-                        ring2(d, s, j).start()
-            value = landed(7)
-            for j in range(2):
-                v = value[j]
-                for d in range(2):
-                    ring2(d, 4, j).wait_recv()
-                    v = v + small_r[d, 6 + j].astype(F32)
-                total[j] = v
-                fin_s[j] = v.astype(BF)
-            last = copy(fin_s.at[1 - x], fin_r.at[1], rs_s, rs_r.at[40], x_next)
+                    landed(2 * s - 3 + d)
+                    for i in (1, 0):
+                        k = (s - 1) * 2 + i
+                        value = piece(2 * s - 3 + d, i)
+                        if s > 2 or i == d:
+                            ring2(d, s - 1, i).wait_recv()
+                            value = value + small_r[d, k - 2].astype(F32)
+                        small_s[d, k] = value.astype(BF)
+                        ring2(d, s, i).start()
+            landed(7)
+            fin_s[0] = piece(7, 1).astype(BF)
+            last = copy(fin_s.at[0], fin_r.at[0], rs_s, rs_r.at[40], x_next)
             last.start()
+            value = piece(7, 0)
+            for d in range(2):
+                for i in range(2):
+                    ring2(d, 4, i).wait_recv()
+                    value = value + small_r[d, 6 + i].astype(F32)
             last.wait_recv()
-            finish(total[x] + fin_r[1].astype(F32))
+            finish(value + fin_r[0].astype(F32))
             sent(big_s.at[pl.ds(0, 63)], rs_s, rs_r.at[0])
 
         turned_copy().wait_send()
-        sent(delta, dl_s, dl_r)
 
 
 def shards(token_states, token_ids, master, gain, cand_ids, slab_owner):
@@ -598,6 +630,9 @@
             V((NZ, NY, 2, 2, 3, 8, emb // 8), BF),
             V((tokens, emb), BF),
             V((tokens, emb), BF),
+            V((tokens, emb), F32),
+            V((seqs, 1, length), jnp.int32),
+            V((3, 8, emb // 8), F32),
             V((NZ, 8, rows, emb), F32),
             V((2, rows, emb), F32),
             V((64, rows, emb), BF),
@@ -618,6 +653,7 @@
             dma, dma((8,)),
             dma, dma,
             dma, dma,
+            dma((2,)), dma((2,)),
             dma, dma((64,)),
         ],
         compiler_params=pltpu.CompilerParams(

time: 91.9 us -> 88.7 us (0.965)
  Pallas kernels: 90.2 us -> 86.9 us
    pallas_call x1, Pallas kernels: 90.2 us -> 86.9 us  [shards(): pl.pallas_call(body, out_shape=jax.ShapeDtypeStruct((rows, emb), F32), in...]
where the time goes in v4:
time: 88.7 us; the launch traced here: 88.5 us
  Pallas kernels  86.9 us (98%)
  local copies, waits for them, and re-layouts  1.57 us (2%)
    pallas_call x1, Pallas kernels, shards(): pl.pallas_call(body, out_shape=jax.ShapeDtypeStruct((rows, emb), F32), in...  86.9 us

profile of v4, /device:TPU:8, one launch (start us, length us, event | category | flops | bytes accessed | tf_op | source)
XLA Modules:
  0.0 88.5 jit_solution(5899092727937729628)
XLA Ops:
  0.0 86.9 %shard_map.64 = f32[32,1024]{1,0:T(8,128)} custom-call(bf16[384,4096]{1,0:T(8,128)(2,1)} %bitcast.6, f32[32,1024]{1,0:T(8,128)} %bitcast.8, f32[1,4096]{1,0:T(1,128)} %bitcast.9, s32[3,1,128]{2,1,0:T(1,128)} %bitcast.11, s32[3,128]{1,0:T(4,128)} %bitcast.10, s32[3,8]{1,0:T(4,128)} %cand_s.1, s32[384]{0:T(512)} %owner_s.1), custom_call_target="tpu_custom_call" | custom-call | tf_op jit(solution)/shard_map/pallas_call | solution.py:613
  86.9 1.6 %copy.8 = f32[1,32,1024]{2,1,0:T(8,128)} copy(f32[1,32,1024]{2,1,0:T(8,128)} %bitcast.7) | data formatting | bytes 262144

commit v5 on v4

--- a/solution.py
+++ b/solution.py
@@ -31,7 +31,7 @@
 def body(
     states_hbm, master_hbm, gain_hbm, ids_ref, owner_ref, cand_s, owner_s, out_ref,
     states, master, gain, normed, trans, trans_peer, weight, wrecv, act, stage, stored, slab,
-    delta, delta_peer, act_peer, ids_peer, stage_peer, part, total, big_s, big_r, x1_s, x1_r, small_s, small_r, fin_s, fin_r, place_s,
+    deltas, act_peer, ids_peer, stage_peer, part, total, big_s, big_r, x1_s, x1_r, small_s, small_r, fin_s, fin_r, place_s,
     ld_sem, ag_s, ag_r, fw_s, fw_r, wt_s, wt_r, tp_s, tp_r,
     e1_s, e1_r, e2_s, e2_r, e3_s, e3_r, dl_s, dl_r, ac_s, ac_r, rs_s, rs_r,
 ):
@@ -380,17 +380,18 @@
             inner = full_sum(pooled[q] * grad)
             scale = scales[q]
             stage[q] = scale * grad - pooled[q] * (scale * scale * scale) * inner * (1.0 / emb)
-        def fill(q, count, mask, act_ref, stage_ref, delta_ref):
+        def fill(q, count, mask, act_ref, stage_ref, base_row):
             span = slice(q * length, (q + 1) * length)
             for k in range(8):
                 cols = slice(k * lanes, (k + 1) * lanes)
                 a = act_ref[span, cols]
                 base = jnp.where(mask, 1.0 / count, 0.0) * stage_ref[q, k : k + 1, :]
-                delta_ref[span, cols] = (base * (1.0 - a * a)).astype(BF)
+                rows = slice(base_row + q * length, base_row + (q + 1) * length)
+                deltas[rows, cols] = (base * (1.0 - a * a)).astype(BF)
 
         grads = copy(stage, stage_peer, dl_s, dl_r, partner)
         for q in range(3):
-            fill(q, counts[q], masks[q], act, stage, delta)
+            fill(q, counts[q], masks[q], act, stage, 0)
             if q == 0:
                 grads.start()
         for pending in act_copies():
@@ -399,15 +400,15 @@
         for q in range(3):
             valid = (ids_peer[q] != 0).astype(jnp.int32)
             count = jnp.sum(valid, axis=1, keepdims=True)
-            fill(q, count.astype(F32), places < count, act_peer, stage_peer, delta_peer)
+            fill(q, count.astype(F32), places < count, act_peer, stage_peer, tokens)
         sent(slab.at[0:7, :, :, 0], e2_s, e2_r.at[0])
         sent(slab.at[:, :, :, c], e3_s, e3_r)
         weight_copy().wait_send()
         turned_copy().wait_recv()
 
         def unit(u, lhs, lhs_peer):
-            value = jnp.dot(lhs.reshape(256, tokens), delta[...], preferred_element_type=F32)
-            value = value + jnp.dot(lhs_peer.reshape(256, tokens), delta_peer[...], preferred_element_type=F32)
+            both = jnp.concatenate([lhs.reshape(256, tokens), lhs_peer.reshape(256, tokens)], axis=1)
+            value = jnp.dot(both, deltas[...], preferred_element_type=F32)
             part[u] = value.reshape(8, 32, emb)
 
         def finish(value):
@@ -512,12 +513,15 @@
 
         @pl.when(c == 1)
         def _():
-            def compute(i, carry):
-                yy = (y + 2 + i // 2) % NY
-                h = i % 2
-                half = pl.ds(h * 4, 4)
-                unit(yy * 2 + h, trans[half, yy, :, 1], trans_peer[half, yy])
-                return carry
+            def compute(off):
+                yy = (y + off) % NY
+
+                def one(h, carry):
+                    half = pl.ds(h * 4, 4)
+                    unit(yy * 2 + h, trans[half, yy, :, 1], trans_peer[half, yy])
+                    return carry
+
+                lax.fori_loop(0, 2, one, 0)
 
             def local(yy, j):
                 zz = (z + RS_OFFS[j]) % NZ
@@ -535,12 +539,11 @@
             def place(d, s, j):
                 return pl.ds(2 * spot(d, s, j), 2)
 
-            lax.fori_loop(0, 2, compute, 0)
-            for j in range(8):
+            def opposite(j):
                 big_s[place(j % 2, 1, j)] = local(y + 2, j).astype(BF)
                 ring(j % 2, 1, j).start()
-            lax.fori_loop(2, NZ, compute, 0)
-            for j in range(8):
+
+            def nearest(j):
                 for d in range(2):
                     value = local(y + STEP[d], j)
                     if j and j % 2 == d:
@@ -548,6 +551,18 @@
                         value = value + big_r[place(d, 1, j)].astype(F32)
                     big_s[place(d, 2, j)] = value.astype(BF)
                     ring(d, 2, j).start()
+
+            compute(2)
+            for j in range(4):
+                opposite(j)
+            compute(3)
+            compute(1)
+            nearest(0)
+            for j in range(4, 8):
+                opposite(j)
+            compute(0)
+            for j in range(1, 4):
+                nearest(j)
 
             def landed(j):
                 if j == 0:
@@ -574,6 +589,8 @@
             for i in range(2):
                 small_s[i, i] = piece(0, i).astype(BF)
                 ring2(i, 1, i).start()
+            for j in range(4, 8):
+                nearest(j)
             for s in range(2, 5):
                 for d in range(2):
                     landed(2 * s - 3 + d)
@@ -628,8 +645,7 @@
             V((3, 8, emb // 8), F32),
             V((3, 8, emb // 8), BF),
             V((NZ, NY, 2, 2, 3, 8, emb // 8), BF),
-            V((tokens, emb), BF),
-            V((tokens, emb), BF),
+            V((2 * tokens, emb), BF),
             V((tokens, emb), F32),
             V((seqs, 1, length), jnp.int32),
             V((3, 8, emb // 8), F32),

time: 88.7 us -> 89.1 us (level)
  no operation moved by 1% of the time
where the time goes in v5:
time: 89.1 us; the launch traced here: 88.3 us
  Pallas kernels  86.7 us (97%)
  local copies, waits for them, and re-layouts  1.57 us (2%)
    pallas_call x1, Pallas kernels, shards(): pl.pallas_call(body, out_shape=jax.ShapeDtypeStruct((rows, emb), F32), in...  86.7 us

profile of v5, /device:TPU:8, one launch (start us, length us, event | category | flops | bytes accessed | tf_op | source)
XLA Modules:
  0.0 88.3 jit_solution(17022449091118783966)
XLA Ops:
  0.0 86.7 %shard_map.64 = f32[32,1024]{1,0:T(8,128)} custom-call(bf16[384,4096]{1,0:T(8,128)(2,1)} %bitcast.6, f32[32,1024]{1,0:T(8,128)} %bitcast.8, f32[1,4096]{1,0:T(1,128)} %bitcast.9, s32[3,1,128]{2,1,0:T(1,128)} %bitcast.11, s32[3,128]{1,0:T(4,128)} %bitcast.10, s32[3,8]{1,0:T(4,128)} %cand_s.1, s32[384]{0:T(512)} %owner_s.1), custom_call_target="tpu_custom_call" | custom-call | tf_op jit(solution)/shard_map/pallas_call | solution.py:630
  86.7 1.6 %copy.8 = f32[1,32,1024]{2,1,0:T(8,128)} copy(f32[1,32,1024]{2,1,0:T(8,128)} %bitcast.7) | data formatting | bytes 262144

commit v6 on v4

--- a/solution.py
+++ b/solution.py
@@ -15,8 +15,7 @@
 AG_XL = (1, 3, 2)
 RS_XL = (1, 3, 2)
 STEP = (1, -1)
-NEAR = (0, 1, -1, 2, -2)
-FAR = (3, -3, 4)
+BATCHES = ((0, 1, -1), (2, -2), (3, -3, 4))
 
 
 def units_of(x_last):
@@ -332,8 +331,8 @@
         for q in range(3):
             stored[q] = units[q].astype(BF)
         weight_copy().wait_recv()
-        for b in (1, 0):
-            for off in (NEAR, FAR)[b]:
+        for b in (2, 1, 0):
+            for off in BATCHES[b]:
                 to = dev(z + off, y, x, c, 0)
                 copy(stored, slab.at[z, y, x, c], e1_s, e1_r.at[b], to).start()
         out_ref[...] = wrecv[...].astype(F32)
@@ -345,14 +344,14 @@
 
         def e2(b, dy, dx):
             to = dev(z, y + dy, (x + dx) % 2, c)
-            for off in (NEAR, FAR)[b]:
+            for off in BATCHES[b]:
                 push(slab.at[(z + off) % NZ, y, x, c], e2_s, e2_r.at[dy * 2 + dx], to)
 
         def e3(yy, xx):
             push(slab.at[:, yy % NY, xx, c], e3_s, e3_r, partner)
 
-        for b in range(2):
-            got(slab.at[0 : len((NEAR, FAR)[b]), y, x, c], e1_s, e1_r.at[b])
+        for b in range(3):
+            got(slab.at[0 : len(BATCHES[b]), y, x, c], e1_s, e1_r.at[b])
             for dy, dx in sends:
                 e2(b, dy, dx)
         e3(y, x)
@@ -649,7 +648,7 @@
             dma, dma,
             dma, dma,
             dma, dma,
-            dma, dma((2,)),
+            dma, dma((3,)),
             dma, dma((8,)),
             dma, dma,
             dma, dma,

time: 88.7 us -> 88.6 us (level)
  no operation moved by 1% of the time
where the time goes in v6:
time: 88.6 us; the launch traced here: 88.4 us
  Pallas kernels  86.9 us (98%)
  local copies, waits for them, and re-layouts  1.57 us (2%)
    pallas_call x1, Pallas kernels, shards(): pl.pallas_call(body, out_shape=jax.ShapeDtypeStruct((rows, emb), F32), in...  86.9 us

profile of v6, /device:TPU:8, one launch (start us, length us, event | category | flops | bytes accessed | tf_op | source)
XLA Modules:
  0.0 88.4 jit_solution(12204713392701837791)
XLA Ops:
  0.0 86.9 %shard_map.64 = f32[32,1024]{1,0:T(8,128)} custom-call(bf16[384,4096]{1,0:T(8,128)(2,1)} %bitcast.6, f32[32,1024]{1,0:T(8,128)} %bitcast.8, f32[1,4096]{1,0:T(1,128)} %bitcast.9, s32[3,1,128]{2,1,0:T(1,128)} %bitcast.11, s32[3,128]{1,0:T(4,128)} %bitcast.10, s32[3,8]{1,0:T(4,128)} %cand_s.1, s32[384]{0:T(512)} %owner_s.1), custom_call_target="tpu_custom_call" | custom-call | tf_op jit(solution)/shard_map/pallas_call | solution.py:612
  86.9 1.6 %copy.8 = f32[1,32,1024]{2,1,0:T(8,128)} copy(f32[1,32,1024]{2,1,0:T(8,128)} %bitcast.7) | data formatting | bytes 262144
